TPU v7x, 32 devices: a whole 2x2x4 slice. The times are simulated.
32 devices in a mesh: dp: 16 (over z, y, x), mp: 2 (over core).
Axes of the slice: x: 2, y: 2, z: 4, core: 2. Of those that a mesh axis runs over, the one named last changes fastest.
Arguments:
- latents: bfloat16 [131072, 1024], P(('dp', 'mp')), may hold values from -6 to 6
- first_scale: float32 [1024], replicated, may hold values from 0.25 to 1.75
- first_shift: float32 [1024], replicated, may hold values from -3 to 3
- input_weights: bfloat16 [3, 1024, 1024], P(None, None, 'mp'), may hold values from -0.1875 to 0.1875
- input_bias: bfloat16 [2, 1024], P(None, 'mp'), may hold values from -1.1953125 to 1.1953125
- output_weight: bfloat16 [1024, 1024], P('mp'), may hold values from -0.75 to 0.75
- output_bias: float32 [1024], replicated, may hold values from -3 to 3
- second_scale: float32 [1024], replicated, may hold values from 0.25 to 1.75
- second_shift: float32 [1024], replicated, may hold values from -3 to 3
- up_weight: bfloat16 [1024, 1024], P(None, 'mp'), may hold values from -0.1875 to 0.1875
- up_bias: bfloat16 [1024], P('mp'), may hold values from -3 to 3
- down_weight: bfloat16 [1024, 1024], P('mp'), may hold values from -0.1875 to 0.1875
- down_bias: float32 [1024], replicated, may hold values from -3 to 3
- output_grad: bfloat16 [131072, 1024], P(('dp', 'mp')), may hold values from -12 to 12
Outputs:
- block_output: float32 [131072, 1024], P(('dp', 'mp'))
- latents_grad: float32 [131072, 1024], P(('dp', 'mp'))
- first_scale_grad: float32 [1024], replicated
- first_shift_grad: float32 [1024], replicated
- input_weights_grad: float32 [3, 1024, 1024], P(None, None, 'mp')
- input_bias_grad: float32 [2, 1024], P(None, 'mp')
- output_weight_grad: float32 [1024, 1024], P('mp')
- output_bias_grad: float32 [1024], replicated
- second_scale_grad: float32 [1024], replicated
- second_shift_grad: float32 [1024], replicated
- up_weight_grad: float32 [1024, 1024], P(None, 'mp')
- up_bias_grad: float32 [1024], P('mp')
- down_weight_grad: float32 [1024, 1024], P('mp')
- down_bias_grad: float32 [1024], replicated
All inputs are finite; a program needn't handle non-finite values.
Results may differ from a plain program's by a relative error of at most 0.02.
Values may be sent and summed in bfloat16 or wider, within the bound.
A program may use at most 384 MiB of HBM per device.

v0:
```python
import jax
import jax.numpy as jnp
from jax import lax
from jax.sharding import PartitionSpec as P

HEAD = 128
LAT = 512
IMG_DEV = 16


EPS = 1e-05
OVER_ROWS = (((0,), (0,)), ((), ()))
OVER_COLUMNS = (((1,), (1,)), ((), ()))


def normalize(values, gain, offset):
    centre = jnp.mean(values, axis=-1, keepdims=True)
    centred = values - centre
    spread = jnp.mean(centred * centred, axis=-1, keepdims=True)
    inverse = lax.rsqrt(spread + EPS)
    unit_rows = centred * inverse
    return (unit_rows, inverse, (unit_rows * gain + offset).astype(jnp.bfloat16))


def normalize_back(upstream, unit_rows, inverse, gain):
    scaled = upstream * gain
    inner = (
        scaled
        - jnp.mean(scaled, axis=-1, keepdims=True)
        - unit_rows * jnp.mean(scaled * unit_rows, axis=-1, keepdims=True)
    )
    return (inverse * inner, jnp.sum(upstream * unit_rows, axis=0), jnp.sum(upstream, axis=0))


def gelu_tanh(values):
    return jax.nn.gelu(values, approximate=True)


def head_scores(image_part, head_count):
    shaped = image_part.reshape(3, LAT, head_count, HEAD)
    scores = jnp.einsum(
        "qhe,khe->hqk", shaped[0], shaped[1], preferred_element_type=jnp.float32
    ) * HEAD ** (-0.5)
    return (shaped, scores)


def attend(heads_in):
    head_width = heads_in.shape[2]
    head_count = head_width // HEAD
    image_count = heads_in.shape[1] // LAT

    def one_image(image_index):
        image_part = lax.dynamic_slice_in_dim(heads_in, image_index * LAT, LAT, 1)
        shaped, scores = head_scores(image_part, head_count)
        highest = jnp.max(scores, axis=-1, keepdims=True)
        log_total = jnp.log(jnp.sum(jnp.exp(scores - highest), axis=-1, keepdims=True)) + highest
        probs_low = jnp.exp(scores - log_total).astype(jnp.bfloat16)
        mixed_part = jnp.einsum(
            "hqk,khe->qhe", probs_low, shaped[2], preferred_element_type=jnp.float32
        )
        return (mixed_part.reshape(LAT, head_width).astype(jnp.bfloat16), log_total)

    mixed_heads, log_totals = lax.map(one_image, jnp.arange(image_count, dtype=jnp.int32))
    return (mixed_heads.reshape(image_count * LAT, head_width), log_totals)


def attend_back(heads_in, log_totals, d_mixed):
    head_width = heads_in.shape[2]
    head_count = head_width // HEAD
    image_count = heads_in.shape[1] // LAT
    head_scale = HEAD ** (-0.5)

    def one_image(image_index, grads_so_far):
        image_part = lax.dynamic_slice_in_dim(heads_in, image_index * LAT, LAT, 1)
        shaped, scores = head_scores(image_part, head_count)
        upstream = lax.dynamic_slice_in_dim(d_mixed, image_index * LAT, LAT, 0).reshape(
            LAT, head_count, HEAD
        )
        probs = jnp.exp(scores - log_totals[image_index])
        d_probs = jnp.einsum(
            "qhe,khe->hqk", upstream, shaped[2], preferred_element_type=jnp.float32
        )
        d_scores = (probs * (d_probs - jnp.sum(d_probs * probs, axis=-1, keepdims=True))).astype(
            jnp.bfloat16
        )
        d_query = (
            jnp.einsum("hqk,khe->qhe", d_scores, shaped[1], preferred_element_type=jnp.float32)
            * head_scale
        )
        d_keys = (
            jnp.einsum("hqk,qhe->khe", d_scores, shaped[0], preferred_element_type=jnp.float32)
            * head_scale
        )
        d_values = jnp.einsum(
            "hqk,qhe->khe", probs.astype(jnp.bfloat16), upstream, preferred_element_type=jnp.float32
        )
        stacked = (
            jnp.stack([d_query, d_keys, d_values]).reshape(3, LAT, head_width).astype(jnp.bfloat16)
        )
        return lax.dynamic_update_slice_in_dim(grads_so_far, stacked, image_index * LAT, 1)

    return lax.fori_loop(0, image_count, one_image, jnp.zeros_like(heads_in))


def per_device(
    latents,
    first_scale,
    first_shift,
    input_weights,
    input_bias,
    output_weight,
    output_bias,
    second_scale,
    second_shift,
    up_weight,
    up_bias,
    down_weight,
    down_bias,
    output_grad,
):
    own_rows = latents.astype(jnp.float32)
    unit_one, inverse_one, normed_one = normalize(own_rows, first_scale, first_shift)
    rows_one = lax.all_gather(normed_one, "mp", axis=0, tiled=True)
    bias_rows = input_bias.astype(jnp.float32)
    bias_three = jnp.stack([bias_rows[0], jnp.zeros_like(bias_rows[0]), bias_rows[1]])[:, None, :]
    heads_in = (
        jnp.einsum("nd,cde->cne", rows_one, input_weights, preferred_element_type=jnp.float32)
        + bias_three
    ).astype(jnp.bfloat16)
    mixed_heads, log_totals = attend(heads_in)
    attention_branch = lax.psum_scatter(
        jnp.dot(mixed_heads, output_weight, preferred_element_type=jnp.float32),
        "mp",
        scatter_dimension=0,
        tiled=True,
    )
    middle = own_rows + attention_branch + output_bias
    unit_two, inverse_two, normed_two = normalize(middle, second_scale, second_shift)
    rows_two = lax.all_gather(normed_two, "mp", axis=0, tiled=True)
    hidden = jnp.dot(rows_two, up_weight, preferred_element_type=jnp.float32) + up_bias.astype(
        jnp.float32
    )
    activated = gelu_tanh(hidden).astype(jnp.bfloat16)
    feed_branch = lax.psum_scatter(
        jnp.dot(activated, down_weight, preferred_element_type=jnp.float32).astype(jnp.bfloat16),
        "mp",
        scatter_dimension=0,
        tiled=True,
    ).astype(jnp.float32)
    block_output = middle + feed_branch + down_bias
    grad_rows = output_grad.astype(jnp.float32)
    grad_all = lax.all_gather(output_grad, "mp", axis=0, tiled=True)
    d_activated = lax.dot_general(
        grad_all, down_weight, OVER_COLUMNS, preferred_element_type=jnp.float32
    )
    g_down_weight = lax.dot_general(
        activated, grad_all, OVER_ROWS, preferred_element_type=jnp.float32
    )
    gelu_pull = jax.vjp(gelu_tanh, hidden)[1]
    d_hidden = gelu_pull(d_activated)[0].astype(jnp.bfloat16)
    g_up_weight = lax.dot_general(rows_two, d_hidden, OVER_ROWS, preferred_element_type=jnp.float32)
    g_up_bias = jnp.sum(d_hidden, axis=0, dtype=jnp.float32)
    d_normed_two = lax.psum_scatter(
        lax.dot_general(d_hidden, up_weight, OVER_COLUMNS, preferred_element_type=jnp.float32),
        "mp",
        scatter_dimension=0,
        tiled=True,
    )
    middle_extra, g_second_scale, g_second_shift = normalize_back(
        d_normed_two, unit_two, inverse_two, second_scale
    )
    d_middle = grad_rows + middle_extra
    d_middle_low = d_middle.astype(jnp.bfloat16)
    middle_all = lax.all_gather(d_middle_low, "mp", axis=0, tiled=True)
    d_mixed = lax.dot_general(
        middle_all, output_weight, OVER_COLUMNS, preferred_element_type=jnp.float32
    ).astype(jnp.bfloat16)
    g_output_weight = lax.dot_general(
        mixed_heads, middle_all, OVER_ROWS, preferred_element_type=jnp.float32
    )
    d_heads = attend_back(heads_in, log_totals, d_mixed)
    g_input_weights = jnp.einsum(
        "nd,cne->cde", rows_one, d_heads, preferred_element_type=jnp.float32
    )
    g_input_bias = jnp.stack(
        [
            jnp.sum(d_heads[0], axis=0, dtype=jnp.float32),
            jnp.sum(d_heads[2], axis=0, dtype=jnp.float32),
        ]
    )
    d_normed_one = lax.psum_scatter(
        jnp.einsum(
            "cne,cde->nd", d_heads, input_weights, preferred_element_type=jnp.float32
        ).astype(jnp.bfloat16),
        "mp",
        scatter_dimension=0,
        tiled=True,
    ).astype(jnp.float32)
    first_extra, g_first_scale, g_first_shift = normalize_back(
        d_normed_one, unit_one, inverse_one, first_scale
    )
    latents_grad = d_middle + first_extra
    g_output_bias = jnp.sum(d_middle, axis=0)
    g_down_bias = jnp.sum(grad_rows, axis=0)
    g_input_weights, g_input_bias, g_output_weight, g_up_weight, g_up_bias, g_down_weight = (
        lax.psum(g_input_weights.astype(jnp.bfloat16), "dp").astype(jnp.float32),
        lax.psum(g_input_bias.astype(jnp.bfloat16), "dp").astype(jnp.float32),
        lax.psum(g_output_weight.astype(jnp.bfloat16), "dp").astype(jnp.float32),
        lax.psum(g_up_weight.astype(jnp.bfloat16), "dp").astype(jnp.float32),
        lax.psum(g_up_bias.astype(jnp.bfloat16), "dp").astype(jnp.float32),
        lax.psum(g_down_weight.astype(jnp.bfloat16), "dp").astype(jnp.float32),
    )
    g_first_scale, g_first_shift, g_output_bias, g_second_scale, g_second_shift, g_down_bias = (
        lax.psum(
            (
                g_first_scale,
                g_first_shift,
                g_output_bias,
                g_second_scale,
                g_second_shift,
                g_down_bias,
            ),
            ("dp", "mp"),
        )
    )
    factor = 1.0 / (IMG_DEV * lax.axis_size("dp"))
    return (
        block_output,
        latents_grad,
        g_first_scale * factor,
        g_first_shift * factor,
        g_input_weights * factor,
        g_input_bias * factor,
        g_output_weight * factor,
        g_output_bias * factor,
        g_second_scale * factor,
        g_second_shift * factor,
        g_up_weight * factor,
        g_up_bias * factor,
        g_down_weight * factor,
        g_down_bias * factor,
    )


def solution(mesh):
    return jax.shard_map(
        per_device,
        mesh=mesh,
        in_specs=(
            P(("dp", "mp"), None),
            P(),
            P(),
            P(None, None, "mp"),
            P(None, "mp"),
            P("mp", None),
            P(),
            P(),
            P(),
            P(None, "mp"),
            P("mp"),
            P("mp", None),
            P(),
            P(("dp", "mp"), None),
        ),
        out_specs=(
            P(("dp", "mp"), None),
            P(("dp", "mp"), None),
            P(),
            P(),
            P(None, None, "mp"),
            P(None, "mp"),
            P("mp", None),
            P(),
            P(),
            P(),
            P(None, "mp"),
            P("mp"),
            P("mp", None),
            P(),
        ),
        check_vma=False,
    )
```

profile of v0, /device:TPU:0, one launch (start us, length us, event | category | flops | bytes accessed | tf_op | source)
XLA Modules:
  0.0 1260.6 jit_solution(13943862512690486486)
XLA Ops:
  24.2 32.2 %all-gather.5.cloned.1.call-done = bf16[8192,1024]{1,0:T(8,128)(2,1)} async-done(((bf16[4096,1024]{1,0:T(8,128)(2,1)}), bf16[8192,1024]{1,0:T(8,128)(2,1)}) %all-gather.5.cloned.1.call-update) | async-done | bytes 16777232 | tf_op jit(solution)/shard_map/all_gather | solution.py:123
  56.4 35.1 %fusion.16 = bf16[3,8192,512]{2,1,0:T(8,128)(2,1)} fusion(f32[3,512]{1,0:T(4,128)S(1)} %pad_maximum_fusion, bf16[3,1024,512]{2,1,0:T(8,128)(2,1)S(1)} %copy-done, bf16[8192,1024]{1,0:T(8,128)(2,1)} %all-gather.5.cloned.1.call-done), kind=kOutput, calls=%fused_computation.35 | convolution fusion | flops 25794969600 | bytes 45094912 | tf_op jit(solution)/shard_map/nd,cde->cne/dot_general | solution.py:127
  91.5 33.4 %copy.48 = bf16[3,8192,512]{1,2,0:T(8,128)(2,1)} copy(bf16[3,8192,512]{2,1,0:T(8,128)(2,1)} %fusion.16) | data formatting | bytes 50331648 | tf_op jit(solution)/shard_map/while | solution.py:63
  124.9 158.1 %while.25 = (s32[]{:T(128)}, bf16[16,512,512]{2,1,0:T(8,128)(2,1)}, f32[16,4,512,1]{2,1,3,0:T(4,128)S(1)}, s32[16]{0:T(128)S(1)}, bf16[3,8192,512]{1,2,0:T(8,128...) while((s32[]{:T(128)}, bf16[16,512,512]{2,1,0:T(8,128)(2,1)}, ...), condition=%wide.region_5.6_spmd, body=%wide.region_2.5_spmd.sunk | while | flops 545519616 | bytes 19988700 | solution.py:63
  283.0 17.8 %fusion.52 = f32[8192,1024]{1,0:T(8,128)} fusion(bf16[8192,512]{1,0:T(8,128)(2,1)} %bitcast.139, bf16[512,1024]{1,0:T(8,128)(2,1)} %param.23), kind=kOutput, calls=%fused_computation.115 | convolution fusion | flops 8589934592 | bytes 42991616 | tf_op jit(solution)/shard_map/dot_general | solution.py:132
  301.1 46.3 %reduce-scatter.5.cloned.1.call-done = f32[4096,1024]{1,0:T(8,128)} async-done(((f32[8192,1024]{1,0:T(8,128)}), f32[4096,1024]{1,0:T(8,128)}) %reduce-scatter.5.cloned.1.call-update) | async-done | bytes 16777232 | tf_op jit(solution)/shard_map/reduce_scatter | solution.py:131
  347.3 9.2 fusion.48
  368.3 30.8 %all-gather.7.cloned.1.call-done = bf16[8192,1024]{1,0:T(8,128)(2,1)} async-done(((bf16[4096,1024]{1,0:T(8,128)(2,1)}), bf16[8192,1024]{1,0:T(8,128)(2,1)}) %all-gather.7.cloned.1.call-update) | async-done | bytes 16777232 | tf_op jit(solution)/shard_map/all_gather | solution.py:139
  399.0 18.4 %fusion.53 = f32[8192,512]{1,0:T(8,128)} fusion(bf16[8192,1024]{1,0:T(8,128)(2,1)} %all-gather.7.cloned.1.call-done, bf16[1024,512]{1,0:T(8,128)(2,1)} %param.27), kind=kOutput, calls=%fused_computation.116 | convolution fusion | flops 8589934592 | bytes 34603008 | tf_op jit(solution)/shard_map/dot_general | solution.py:140
  417.4 14.3 %all-gather.9.cloned.1.call-done = bf16[8192,1024]{1,0:T(8,128)(2,1)} async-done(((bf16[4096,1024]{1,0:T(8,128)(2,1)}), bf16[8192,1024]{1,0:T(8,128)(2,1)}) %all-gather.9.cloned.1.call-update) | async-done | bytes 16777232 | tf_op jit(solution)/shard_map/all_gather | solution.py:152
  431.7 27.1 %fusion.45 = (bf16[512]{0:T(512)(128)(2,1)}, bf16[8192,512]{1,0:T(8,128)(2,1)}) fusion(f32[8192,512]{1,0:T(8,128)} %fusion.53, f32[512]{0:T(512)S(1)} %convert_element_type.136, bf16[8192,1024]{1,0:T(8,128)(2,1)} %all-gather.9.cloned.1.call-done, bf16[512,1024]{1,0:T(8,128)(2,1)} %param.29), kind=kOutput, calls=%fused_computation.110 | convolution fusion | flops 8682209280 | bytes 42994688 | tf_op jit(solution)/shard_map/dot_general | solution.py:153
  458.8 18.9 %fusion.54 = f32[8192,1024]{1,0:T(8,128)} fusion(bf16[8192,512]{1,0:T(8,128)(2,1)} %get-tuple-element.227, bf16[1024,512]{1,0:T(8,128)(2,1)S(1)} %copy-done.21), kind=kOutput, calls=%fused_computation.117 | convolution fusion | flops 8589934592 | bytes 42991616 | tf_op jit(solution)/shard_map/dot_general | solution.py:164
  477.9 20.1 %convolution_convert_fusion = bf16[8192,1024]{1,0:T(8,128)(2,1)} fusion(bf16[512,1024]{1,0:T(8,128)(2,1)} %param.29, f32[8192,512]{1,0:T(8,128)} %fusion.53, f32[512]{0:T(512)S(1)} %convert_element_type.136), kind=kOutput, calls=%fused_computation.79 | convolution fusion | flops 8640266240 | bytes 34605056 | tf_op jit(solution)/shard_map/dot_general | solution.py:145
  498.0 26.3 %reduce-scatter.9.cloned.1.call-done = f32[4096,1024]{1,0:T(8,128)} async-done(((f32[8192,1024]{1,0:T(8,128)}), f32[4096,1024]{1,0:T(8,128)}) %reduce-scatter.9.cloned.1.call-update) | async-done | bytes 16777232 | tf_op jit(solution)/shard_map/reduce_scatter | solution.py:163
  524.3 14.5 %multiply_reduce_fusion.2 = (f32[1024]{0:T(1024)}, f32[4096]{0:T(1024)S(1)}, f32[4096]{0:T(1024)S(1)}, f32[1024]{0:T(1024)}) fusion(f32[4096,1024]{1,0:T(8,128)} %reduce-scatter.9.cloned.1.call-done, f32[4096,1024]{1,0:T(8,128)} %copy-done.1, f32[4096]{0:T(1024)S(1)} %add_rsqrt_fusion, f32[4096]{0:T(1024)S(1)} %broadcast_multiply_fusion.4, f32[1024]{0:T(1024)S(1)} %copy-done.6), kind=kLoop, calls=%fused_computation.72 | loop fusion | flops 37738496 | bytes 33632256 | tf_op jit(solution)/shard_map/reduce_sum | solution.py:32
  538.8 15.1 %reduce-scatter.7.cloned.1.call-done = bf16[4096,1024]{1,0:T(8,128)(2,1)} async-done(((bf16[8192,1024]{1,0:T(8,128)(2,1)}), bf16[4096,1024]{1,0:T(8,128)(2,1)}) %reduce-scatter.7.cloned.1.call-update) | async-done | bytes 8388624 | tf_op jit(solution)/shard_map/reduce_scatter | solution.py:144
  553.9 28.1 %fusion.47 = (f32[1024]{0:T(1024)}, f32[4096,1024]{1,0:T(8,128)}, f32[4096,1024]{1,0:T(8,128)}, f32[1024]{0:T(1024)}) fusion(f32[4096]{0:T(1024)S(1)} %get-tuple-element.246, f32[4096,1024]{1,0:T(8,128)} %copy-done.1, f32[4096]{0:T(1024)S(1)} %broadcast_multiply_fusion.4, f32[4096]{0:T(1024)S(1)} %get-tuple-element.247, ...), kind=kLoop, calls=%fused_computation.111 | loop fusion | flops 58718208 | bytes 83968000 | tf_op jit(solution)/shard_map/reduce_sum | solution.py:203
  582.0 9.1 convert_element_type.142
  591.1 15.6 %convolution_convert_fusion.3 = bf16[1024,512]{1,0:T(8,128)(2,1)} fusion(bf16[8192,1024]{1,0:T(8,128)(2,1)} %all-gather.7.cloned.1.call-done, bf16[8192,512]{1,0:T(8,128)(2,1)} %get-tuple-element.227), kind=kOutput, calls=%fused_computation.90 | convolution fusion | flops 8590458880 | bytes 26214400 | tf_op jit(solution)/shard_map/dot_general | solution.py:161
  606.7 22.8 %convolution_convert_fusion.2 = bf16[512,1024]{1,0:T(8,128)(2,1)} fusion(bf16[8192,1024]{1,0:T(8,128)(2,1)} %all-gather.9.cloned.1.call-done, f32[8192,512]{1,0:T(8,128)} %fusion.53, f32[512]{0:T(512)S(1)} %convert_element_type.136), kind=kOutput, calls=%fused_computation.89 | convolution fusion | flops 8632401920 | bytes 34605056 | tf_op jit(solution)/shard_map/dot_general | solution.py:156
  629.5 14.9 %convolution_convert_fusion.1 = bf16[8192,512]{1,0:T(8,128)(2,1)} fusion(bf16[8192,1024]{1,0:T(8,128)(2,1)} %all-gather.11.cloned.1.call-done, bf16[512,1024]{1,0:T(8,128)(2,1)} %param.23), kind=kOutput, calls=%fused_computation.81 | convolution fusion | flops 8594128896 | bytes 26214400 | tf_op jit(solution)/shard_map/dot_general | solution.py:175
  644.5 8.4 broadcast_in_dim.16
  652.9 236.8 %while.26 = (s32[]{:T(128)}, bf16[3,8192,512]{1,2,0:T(8,128)(2,1)}, bf16[3,8192,512]{1,2,0:T(8,128)(2,1)}, f32[16,4,512,1]{2,1,3,0:T(4,128)}, bf16[8192,512]{1,0...) while((s32[]{:T(128)}, bf16[3,8192,512]{1,2,0:T(8,128)(2,1)}, ...), condition=%wide.region_15.16_spmd, body=%wide.region_13.15_spmd.sunk | while | flops 1360787456 | bytes 45146324 | solution.py:102
  889.7 15.8 %convolution_convert_fusion.4 = bf16[512,1024]{1,0:T(8,128)(2,1)} fusion(bf16[8192,512]{1,0:T(8,128)(2,1)} %bitcast.140, bf16[8192,1024]{1,0:T(8,128)(2,1)} %all-gather.11.cloned.1.call-done), kind=kOutput, calls=%fused_computation.91 | convolution fusion | flops 8590458880 | bytes 26214400 | tf_op jit(solution)/shard_map/dot_general | solution.py:178
  905.5 33.0 %convert_bitcast_fusion = bf16[3,1024,512]{1,2,0:T(8,128)(2,1)} fusion(bf16[3,8192,512]{1,2,0:T(8,128)(2,1)} %get-tuple-element.138, bf16[8192,1024]{1,0:T(8,128)(2,1)} %all-gather.5.cloned.1.call-done), kind=kOutput, calls=%fused_computation.85 | convolution fusion | flops 25771376640 | bytes 45088768 | tf_op jit(solution)/shard_map/nd,cne->cde/dot_general | solution.py:182
  938.6 32.2 %bitcast_convert_fusion = bf16[8192,1024]{1,0:T(8,128)(2,1)} fusion(bf16[3,8192,512]{1,2,0:T(8,128)(2,1)} %get-tuple-element.138, bf16[3,1024,512]{2,1,0:T(8,128)(2,1)S(1)} %copy-done), kind=kOutput, calls=%fused_computation.34 | convolution fusion | flops 25778192384 | bytes 45088768 | tf_op jit(solution)/shard_map/cne,cde->nd/dot_general | solution.py:192
  970.9 7.7 slice_reduce_fusion.1
  978.7 43.3 %all-reduce.1 = (bf16[2,512]{1,0:T(2,128)(2,1)S(1)}, bf16[512]{0:T(512)(128)(2,1)S(1)}) all-reduce(bf16[2,512]{1,0:T(2,128)(2,1)S(1)} %pad_maximum_fusion.1, bf16[512]{0:T(512)(128)(2,1)S(1)} %copy-done.20), channel_id=1, replica_groups=mesh['dp'=16,'mp'=2] {'dp'}, use_global_device_ids=true, to_apply=%region_26.27 | all-reduce | flops 1536 | bytes 6144 | tf_op jit(solution)/shard_map/psum | solution.py:207
  1023.2 129.8 %all-reduce.5.cloned.1.call-done = (bf16[3,1024,512]{1,2,0:T(8,128)(2,1)}, bf16[512,1024]{1,0:T(8,128)(2,1)}, bf16[1024,512]{1,0:T(8,128)(2,1)}, bf16[512,1024]{1,0:T(8,128)(2,1)}) async-done(((bf16[3,1024,512]{1,2,0:T(8,128)(2,1)}, bf16[512,1024]{1,0:T(8,128)(2,1)}, bf16[1024,512]{1,0:T(8,128)(2,1)}, bf16[512,1024]{1,0:T(8,128)(2,1)}), (bf16[3,1024,512]{1,2,0:T(8,128)(2,1)}, bf16[512,1024]{1,0:T(8,128)(2,1)}, ...) | async-done | bytes 6291472 | tf_op jit(solution)/shard_map/psum | solution.py:206
  1181.3 10.3 fusion.39
  1191.6 41.3 %all-reduce = (f32[1024]{0:T(1024)S(1)}, f32[1024]{0:T(1024)S(1)}, f32[1024]{0:T(1024)S(1)}, f32[1024]{0:T(1024)S(1)}, f32[1024]{0:T(1024)S(1)}, /*index=5*/f32[1024]{0:T(1024)S(1)}) all-reduce(f32[1024]{0:T(1024)S(1)} %get-tuple-element.186, f32[1024]{0:T(1024)S(1)} %get-tuple-element.191, ...), channel_id=1, replica_groups=mesh['dp'=16,'mp'=2] {'dp','mp'}, use_global_device_ids=true, to_apply=%region_20.21 | all-reduce | flops 6144 | bytes 49152 | tf_op jit(solution)/shard_map/psum | solution.py:214
  1236.5 17.3 %fusion.28 = f32[4096,1024]{1,0:T(8,128)} fusion(f32[4096,1024]{1,0:T(8,128)} %get-tuple-element.229, bf16[4096,1024]{1,0:T(8,128)(2,1)} %param.18, bf16[4096,1024]{1,0:T(8,128)(2,1)} %reduce-scatter.11.cloned.1.call-done, f32[4096]{0:T(1024)S(1)} %broadcast_multiply_fusion, f32[4096]{0:T(1024)S(1)} %broadcast_multiply_fusion.1, f32[1024]{0:T(1024)S(1)} %copy-done.8, ...), kind=kLoop, calls=%fused_computation.57 | loop fusion | flops 41943040 | bytes 50401280 | tf_op jit(solution)/shard_map/add | solution.py:202
  (408 shorter events, 445.7 us)
Async XLA Ops:
  7.2 49.2 %copy-start = (bf16[3,1024,512]{2,1,0:T(8,128)(2,1)S(1)}, bf16[3,1024,512]{2,1,0:T(8,128)(2,1)}, u32[]{:S(2)}) copy-start(bf16[3,1024,512]{2,1,0:T(8,128)(2,1)} %param.21) | copy-start | bytes 9437188
  7.2 11.1 copy-start.7
  7.2 11.1 copy-start.18
  7.2 49.1 %all-gather.5.cloned.1.call-start = ((), (), s32[]{:S(2)}) async-start(), calls=%async_computation.4 | async-start | bytes 25165824 | tf_op jit(solution)/shard_map/all_gather | solution.py:123
  7.3 11.0 slice-start
  12.0 5.7 copy-start.2
  12.0 6.3 slice-start.1
  12.0 12.1 copy-start.14
  23.4 323.9 %reduce-scatter.5.cloned.1.call-start = ((), (), s32[]{:S(2)}) async-start(), calls=%async_computation.5 | async-start | bytes 50331648 | tf_op jit(solution)/shard_map/reduce_scatter | solution.py:131
  283.0 17.8 %copy-start.13 = (f32[16,4,512,1]{2,1,3,0:T(4,128)}, f32[16,4,512,1]{2,1,3,0:T(4,128)S(1)}, u32[]{:S(2)}) copy-start(f32[16,4,512,1]{2,1,3,0:T(4,128)S(1)} %get-tuple-element.370) | copy-start | bytes 393220
  300.8 46.5 %copy-start.15 = (f32[1024]{0:T(1024)S(1)}, f32[1024]{0:T(1024)}, u32[]{:S(2)}) copy-start(f32[1024]{0:T(1024)} %param.24) | copy-start | bytes 12292
  300.8 98.2 %all-gather.7.cloned.1.call-start = ((), (), s32[]{:S(2)}) async-start(), calls=%async_computation.6 | async-start | bytes 25165824 | tf_op jit(solution)/shard_map/all_gather | solution.py:139
  356.6 6.2 copy-start.1
  356.6 6.2 copy-start.6
  356.6 6.1 copy-start.16
  362.8 5.5 copy-start.19
  367.6 64.1 %all-gather.9.cloned.1.call-start = ((), (), s32[]{:S(2)}) async-start(), calls=%async_computation.8 | async-start | bytes 25165824 | tf_op jit(solution)/shard_map/all_gather | solution.py:152
  368.2 156.1 %reduce-scatter.9.cloned.1.call-start = ((), (), s32[]{:S(2)}) async-start(), calls=%async_computation.9 | async-start | bytes 50331648 | tf_op jit(solution)/shard_map/reduce_scatter | solution.py:163
  431.7 27.1 %copy-start.21 = (bf16[1024,512]{1,0:T(8,128)(2,1)S(1)}, bf16[1024,512]{1,0:T(8,128)(2,1)}, u32[]{:S(2)}) copy-start(bf16[1024,512]{1,0:T(8,128)(2,1)} %param.27) | copy-start | bytes 3145732
  477.8 76.1 %reduce-scatter.7.cloned.1.call-start = ((), (), s32[]{:S(2)}) async-start(), calls=%async_computation.7 | async-start | bytes 25165824 | tf_op jit(solution)/shard_map/reduce_scatter | solution.py:144
  498.0 55.9 %copy-start.17 = (f32[1024]{0:T(1024)S(1)}, f32[1024]{0:T(1024)}, u32[]{:S(2)}) copy-start(f32[1024]{0:T(1024)} %param.30) | copy-start | bytes 12292
  498.0 131.6 %all-gather.11.cloned.1.call-start = ((), (), s32[]{:S(2)}) async-start(), calls=%async_computation.10 | async-start | bytes 25165824 | tf_op jit(solution)/shard_map/all_gather | solution.py:174
  591.1 561.9 %all-reduce.5.cloned.1.call-start = ((), (), s32[]{:S(2)}) async-start(), calls=%async_computation.12 | async-start | bytes 12582912 | tf_op jit(solution)/shard_map/psum | solution.py:206
  938.6 242.7 %reduce-scatter.11.cloned.1.call-start = ((), (), s32[]{:S(2)}) async-start(), calls=%async_computation.11 | async-start | bytes 25165824 | tf_op jit(solution)/shard_map/reduce_scatter | solution.py:191
  970.9 7.8 copy-start.20
  978.6 202.6 %copy-start.3 = (f32[4096]{0:T(1024)S(1)}, f32[4096]{0:T(1024)}, u32[]{:S(2)}) copy-start(f32[4096]{0:T(1024)} %copy-done.2) | copy-start | bytes 49156
  978.6 202.6 %copy-start.5 = (f32[4096]{0:T(1024)S(1)}, f32[4096]{0:T(1024)}, u32[]{:S(2)}) copy-start(f32[4096]{0:T(1024)} %copy-done.4) | copy-start | bytes 49156
  978.6 202.6 %copy-start.8 = (f32[1024]{0:T(1024)S(1)}, f32[1024]{0:T(1024)}, u32[]{:S(2)}) copy-start(f32[1024]{0:T(1024)} %param.19) | copy-start | bytes 12292
  1158.4 33.1 %copy-start.9 = (f32[1024]{0:T(1024)S(1)}, f32[1024]{0:T(1024)}, u32[]{:S(2)}) copy-start(f32[1024]{0:T(1024)} %get-tuple-element.182) | copy-start | bytes 12292
  1158.5 33.1 %copy-start.10 = (f32[1024]{0:T(1024)S(1)}, f32[1024]{0:T(1024)}, u32[]{:S(2)}) copy-start(f32[1024]{0:T(1024)} %get-tuple-element.189) | copy-start | bytes 12292
  1158.5 33.1 %copy-start.11 = (f32[1024]{0:T(1024)S(1)}, f32[1024]{0:T(1024)}, u32[]{:S(2)}) copy-start(f32[1024]{0:T(1024)} %get-tuple-element.228) | copy-start | bytes 12292
  1158.5 33.1 %copy-start.12 = (f32[1024]{0:T(1024)S(1)}, f32[1024]{0:T(1024)}, u32[]{:S(2)}) copy-start(f32[1024]{0:T(1024)} %get-tuple-element.243) | copy-start | bytes 12292
  (1 other events, 0.6 us)
Sparse Core Ops, SparseCore 0:
  23.6 32.7 all-gather.4
  301.0 46.3 reduce-scatter.4
  367.7 31.2 all-gather.6
  400.4 31.2 all-gather.8
  477.9 46.3 reduce-scatter.8
  526.4 27.3 reduce-scatter.6
  591.2 31.2 all-gather.10
  938.7 214.2 all-reduce.4
  1156.0 25.2 reduce-scatter.10
where the time goes:
time: 1270 us; the launch traced here: 1260 us
  matrix products  411 us (32%)
  waiting for transfers between devices  302 us (24%)
  local copies, waits for them, and re-layouts  246 us (19%)
  other arithmetic  190 us (15%)
  blocking collectives  84.6 us (7%)
  between operations  14.5 us (1%)
    psum x1, waiting for transfers between devices, per_device(): lax.psum(g_input_weights.astype(jnp.bfloat16), 'dp').astype(jnp.float32)  130 us
    dynamic_update_slice x32, local copies, waits for them, and re-layouts, attend(): lax.map(one_image, jnp.arange(image_count, dtype=jnp.int32))  62.9 us
    dynamic_slice x32, local copies, waits for them, and re-layouts, one_image(): lax.dynamic_slice_in_dim(d_mixed, image_index * LAT, LAT, 0)  62.6 us
    reduce_scatter x1, waiting for transfers between devices, per_device(): lax.psum_scatter(jnp.dot(mixed_heads, output_weight, preferred_element_ty...  46.3 us
    psum x1, blocking collectives, per_device(): lax.psum(g_input_bias.astype(jnp.bfloat16), 'dp').astype(jnp.float32)  43.3 us
    psum x1, blocking collectives, per_device(): lax.psum((g_first_scale, g_first_shift, g_output_bias, g_second_scale, g_...  41.3 us
    dot_general x1, matrix products, per_device(): jnp.einsum('nd,cde->cne', rows_one, input_weights, preferred_element_type...  35.1 us
    dot_general x16, matrix products, one_image(): jnp.einsum('qhe,khe->hqk', upstream, shaped[2], preferred_element_type=jn...  35 us
  transfers between devices with their start and end apart: 9, of which 8 were waited for; matrix products, arithmetic and copies ran while one was open for 12% of the time, Pallas kernels for 0%

commit v1 on v0

v1 whole, which is shorter than its diff:
```python
import functools

import jax
import jax.numpy as jnp
from jax import lax
from jax.experimental import pallas as pl
from jax.experimental.pallas import tpu as pltpu
from jax.sharding import PartitionSpec as P

D = 1024
HEAD = 128
HEADS = 8
LAT = 512
HALF = 512
GROUPS = 2
EPS = 1e-05
SCALE = HEAD ** (-0.5)
LOG2E = 1.4426950408889634
GELU_A = 0.7978845608028654
GELU_B = 0.044715
MESH = pl.DeviceIdType.MESH
NN = (((1,), (0,)), ((), ()))
NT = (((1,), (1,)), ((), ()))
TN = (((0,), (0,)), ((), ()))
BF = jnp.bfloat16
F32 = jnp.float32
VMEM_LIMIT = 60 << 20


def mul(a, b, dims):
    return lax.dot_general(a, b, dims, preferred_element_type=F32)


def unit_of(rows):
    centred = rows - jnp.mean(rows, axis=-1, keepdims=True)
    inverse = lax.rsqrt(jnp.mean(centred * centred, axis=-1, keepdims=True) + EPS)
    return centred * inverse, inverse


def norm_back(upstream, unit, inverse, gain):
    scaled = upstream * gain
    inner = (
        scaled
        - jnp.mean(scaled, axis=-1, keepdims=True)
        - unit * jnp.mean(scaled * unit, axis=-1, keepdims=True)
    )
    return inverse * inner


def column_sum(values):
    return jnp.sum(values, axis=0, keepdims=True)


def row_spec(width):
    return pl.BlockSpec((LAT, width), lambda i: (i, 0))


def whole_spec(shape):
    return pl.BlockSpec(shape, lambda *_: (0,) * len(shape), pipeline_mode=pl.Buffered(1))


def kept_spec(shape):
    return pl.BlockSpec(shape, lambda *_: (0,) * len(shape))


ANY = pl.BlockSpec(memory_space=pl.ANY)


def shape_of(shape, dtype):
    return jax.ShapeDtypeStruct(shape, dtype)


def cost(flops, moved):
    return pl.CostEstimate(flops=int(flops), bytes_accessed=int(moved), transcendentals=0)


def dp_flip(bit):
    me = lax.axis_index("dp")
    step = 1 << bit
    on = lax.rem(me // step, 2)
    return (me + step - 2 * step * on, lax.axis_index("mp"))


def core_flip():
    return (lax.axis_index("dp"), 1 - lax.axis_index("mp"))


def greet(partners):
    barrier = pltpu.get_barrier_semaphore()
    for partner in partners:
        pl.semaphore_signal(barrier, inc=1, device_id=partner, device_id_type=MESH)
    pl.semaphore_wait(barrier, len(partners))


def remote(src, dst, send, recv, partner):
    return pltpu.make_async_remote_copy(
        src_ref=src,
        dst_ref=dst,
        send_sem=send,
        recv_sem=recv,
        device_id=partner,
        device_id_type=MESH,
    )


class Reduction:
    def __init__(self, rows, columns, parts, orders):
        self.rows, self.columns, self.parts, self.orders = rows, columns, parts, orders
        self.bits = len(orders[0])
        self.ticks = 2 * self.bits + 2

    def scratch(self):
        stages = 2 * self.bits
        return [
            pltpu.VMEM((self.rows, self.columns), BF),
            pltpu.VMEM((self.rows, self.columns), BF),
            pltpu.VMEM((self.rows, self.columns), BF),
            pltpu.SemaphoreType.DMA((2,)),
            pltpu.SemaphoreType.DMA((len(self.parts), stages)),
            pltpu.SemaphoreType.DMA((len(self.parts), stages)),
        ]

    def offset(self, part, level):
        me = lax.axis_index("dp")
        row = 0
        for stage in range(level):
            on = lax.rem(me // (1 << self.orders[part][stage]), 2)
            row = row + on * (self.rows >> (stage + 1))
        return row

    def aligned(self, row, size):
        return pl.ds(pl.multiple_of(row, size), size)

    def columns_of(self, part):
        first, last = self.parts[part]
        return pl.ds(first, last - first)

    def halving(self, refs, part, stage):
        cur, _, recv, _, send_sem, recv_sem = refs
        size = self.rows >> (stage + 1)
        bit = self.orders[part][stage]
        on = lax.rem(lax.axis_index("dp") // (1 << bit), 2)
        base = self.offset(part, stage)
        cols = self.columns_of(part)
        landing = self.rows - 2 * size
        copy = remote(
            cur.at[self.aligned(base + (1 - on) * size, size), cols],
            recv.at[pl.ds(landing, size), cols],
            send_sem.at[part, stage],
            recv_sem.at[part, stage],
            dp_flip(bit),
        )
        return copy, self.aligned(base + on * size, size), pl.ds(landing, size), cols

    def doubling(self, refs, part, step):
        _, full, _, _, send_sem, recv_sem = refs
        stage = self.bits - 1 - step
        size = self.rows >> (stage + 1)
        rows = self.aligned(self.offset(part, stage + 1), size)
        cols = self.columns_of(part)
        return remote(
            full.at[rows, cols],
            full.at[rows, cols],
            send_sem.at[part, self.bits + step],
            recv_sem.at[part, self.bits + step],
            dp_flip(self.orders[part][stage]),
        )

    def exchange(self, refs, other):
        return remote(other, refs[1], refs[3].at[0], refs[3].at[1], core_flip())

    def tick(self, refs, tick, other):
        cur, landed, recv = refs[:3]
        parts = range(len(self.parts))
        if tick == 0:
            self.exchange(refs, other).start()
            return
        if tick == 1:
            self.exchange(refs, other).wait()
            cur[...] = (cur[...].astype(F32) + landed[...].astype(F32)).astype(BF)
            for part in parts:
                self.halving(refs, part, 0)[0].start()
            return
        if tick <= self.bits + 1:
            for part in parts:
                copy, keep, landing, cols = self.halving(refs, part, tick - 2)
                copy.wait()
                total = (cur[keep, cols].astype(F32) + recv[landing, cols].astype(F32)).astype(BF)
                if tick <= self.bits:
                    cur[keep, cols] = total
                    self.halving(refs, part, tick - 1)[0].start()
                else:
                    landed[keep, cols] = total
                    self.doubling(refs, part, 0).start()
            return
        step = tick - self.bits - 2
        for part in parts:
            self.doubling(refs, part, step).wait()
            if step + 1 < self.bits:
                self.doubling(refs, part, step + 1).start()


ORDERS = ((0, 1, 2, 3), (1, 2, 3, 0), (2, 3, 0, 1))


def reduction_partners():
    return [core_flip()] + [dp_flip(bit) for bit in range(4)]


def first_kernel(
    spread, x_ref, gain_ref, shift_ref, bias_ref, w_in, *refs
):
    step = pl.program_id(0)
    if spread:
        sources = (w_in_any, w_out, w_up, w_down, bias_all) = refs[:5]
        normed_ref, heads_ref = refs[5:7]
        targets = refs[7:12]
        send_sem, recv_sem = refs[12:14]

        def copies():
            return [
                remote(src, dst, send_sem.at[n], recv_sem.at[n], core_flip())
                for n, (src, dst) in enumerate(zip(sources, targets))
            ]

        @pl.when(step == 0)
        def _():
            greet([core_flip()])
            for copy in copies():
                copy.start()
    else:
        normed_ref, heads_ref = refs

    unit, _ = unit_of(x_ref[...].astype(F32))
    normed_ref[...] = (unit * gain_ref[...] + shift_ref[...]).astype(BF)
    project(normed_ref, w_in, bias_ref, heads_ref)

    if spread:

        @pl.when(step == pl.num_programs(0) - 1)
        def _():
            for copy in copies():
                copy.wait()


def project(normed_ref, weights, bias_ref, heads_ref):
    for which in range(3):
        rows = mul(normed_ref[...], weights[which], NN)
        if which != 1:
            place = 0 if which == 0 else 1
            rows = rows + bias_ref[place : place + 1, :].astype(F32)
        heads_ref[which] = rows.astype(BF)


def forward_kernel(
    x_ref,
    normed_ref,
    own_ref,
    g_ref,
    w_in,
    in_bias,
    wo_own,
    wo_other,
    out_bias,
    gain_ref,
    shift_ref,
    wu_own,
    wu_other,
    ub_own,
    ub_other,
    wd_own,
    wd_other,
    down_bias,
    block_ref,
    other_ref,
    probs_ref,
    inv_ref,
    mixed_ref,
    middle_ref,
    slope_ref,
    gdown_ref,
    gsum_ref,
    acc,
    normed_two,
    act,
    wide,
):
    step = pl.program_id(0)

    @pl.when(step == 0)
    def _():
        acc[...] = jnp.zeros_like(acc)
        gsum_ref[...] = jnp.zeros_like(gsum_ref)

    project(normed_ref, w_in, in_bias, other_ref)
    lane = lax.broadcasted_iota(jnp.int32, (LAT, HEAD), 1)
    inverses = jnp.zeros((LAT, HEAD), F32)
    for half, heads_ref in enumerate((own_ref, other_ref)):
        for head in range(HALF // HEAD):
            cols = slice(head * HEAD, (head + 1) * HEAD)
            scores = mul(heads_ref[0, :, cols], heads_ref[1, :, cols], NT)
            highest = jnp.max(scores, axis=-1, keepdims=True)
            powers = jnp.exp2((scores - highest) * (SCALE * LOG2E))
            inverse = 1.0 / jnp.sum(powers, axis=-1, keepdims=True)
            low = powers.astype(BF)
            probs_ref[half, head] = low
            mixed = mul(low, heads_ref[2, :, cols], NN) * inverse
            mixed_ref[half, :, cols] = mixed.astype(BF)
            inverses = jnp.where(lane == half * 4 + head, inverse, inverses)
    inv_ref[...] = inverses
    for chunk in range(4):
        cols = slice(chunk * 256, (chunk + 1) * 256)
        wide[:, cols] = (
            x_ref[:, cols].astype(F32)
            + mul(mixed_ref[0], wo_own[:, cols], NN)
            + mul(mixed_ref[1], wo_other[:, cols], NN)
            + out_bias[:, cols]
        )
    middle = wide[...]
    middle_ref[...] = middle.astype(BF)
    unit, _ = unit_of(middle)
    normed_two[...] = (unit * gain_ref[...] + shift_ref[...]).astype(BF)
    for half, (weight, bias) in enumerate(((wu_own, ub_own), (wu_other, ub_other))):
        for chunk in range(2):
            cols = slice(chunk * 256, (chunk + 1) * 256)
            hidden = mul(normed_two[...], weight[:, cols], NN) + bias[:, cols].astype(F32)
            square = hidden * hidden
            gate = jnp.tanh(GELU_A * (hidden + GELU_B * (square * hidden)))
            lift = 0.5 * (1.0 + gate)
            act[half, :, cols] = (hidden * lift).astype(BF)
            slope = lift + (0.5 * GELU_A) * hidden * (1.0 - gate * gate) * (
                1.0 + (3.0 * GELU_B) * square
            )
            slope_ref[half, :, cols] = slope.astype(BF)
    for chunk in range(4):
        cols = slice(chunk * 256, (chunk + 1) * 256)
        block_ref[:, cols] = (
            wide[:, cols]
            + mul(act[0], wd_own[:, cols], NN)
            + mul(act[1], wd_other[:, cols], NN)
            + down_bias[:, cols]
        )
    for half in range(2):
        acc[half] += mul(act[half], g_ref[...], TN)
    gsum_ref[0:1, :] += column_sum(g_ref[...].astype(F32))

    @pl.when(step == pl.num_programs(0) - 1)
    def _():
        gdown_ref[...] = acc[...].astype(BF)


def feed_back_kernel(
    g_ref,
    slope_ref,
    middle_ref,
    mixed_ref,
    inv_ref,
    wd_own,
    wd_other,
    wu_own,
    wu_other,
    wo_own,
    wo_other,
    gain_ref,
    shift_ref,
    dmid_ref,
    dmix_ref,
    dot_ref,
    gup_ref,
    gout_ref,
    vec_ref,
    ubias_ref,
    acc_up,
    acc_out,
    normed_two,
    unit_ref,
    dhid,
    wide,
):
    step = pl.program_id(0)

    @pl.when(step == 0)
    def _():
        acc_up[...] = jnp.zeros_like(acc_up)
        acc_out[...] = jnp.zeros_like(acc_out)
        vec_ref[...] = jnp.zeros_like(vec_ref)
        ubias_ref[...] = jnp.zeros_like(ubias_ref)

    for half, weight in enumerate((wd_own, wd_other)):
        for chunk in range(2):
            cols = slice(chunk * 256, (chunk + 1) * 256)
            down = mul(g_ref[...], weight[cols, :], NT)
            dhid[half, :, cols] = (down * slope_ref[half, :, cols].astype(F32)).astype(BF)
        ubias_ref[half : half + 1, :] += column_sum(dhid[half].astype(F32))
    unit, inverse = unit_of(middle_ref[...].astype(F32))
    unit_ref[...] = unit
    normed_two[...] = (unit * gain_ref[...] + shift_ref[...]).astype(BF)
    for half in range(2):
        acc_up[half] += mul(dhid[half], normed_two[...], TN)
    for chunk in range(4):
        rows = slice(chunk * 256, (chunk + 1) * 256)
        wide[:, rows] = mul(dhid[0], wu_own[rows, :], NT) + mul(dhid[1], wu_other[rows, :], NT)
    upstream = wide[...]
    unit = unit_ref[...]
    vec_ref[0:1, :] += column_sum(upstream * unit)
    vec_ref[1:2, :] += column_sum(upstream)
    dmid = g_ref[...].astype(F32) + norm_back(upstream, unit, inverse, gain_ref[...])
    vec_ref[2:3, :] += column_sum(dmid)
    dmid_ref[...] = dmid.astype(BF)
    lane = lax.broadcasted_iota(jnp.int32, (LAT, HEAD), 1)
    dots = jnp.zeros((LAT, HEAD), F32)
    for half, weight in enumerate((wo_own, wo_other)):
        acc_out[half] += mul(mixed_ref[half], dmid_ref[...], TN)
        for pair in range(2):
            both = mul(dmid_ref[...], weight[pair * 256 : (pair + 1) * 256, :], NT)
            for one in range(2):
                head = pair * 2 + one
                cols = slice(head * HEAD, (head + 1) * HEAD)
                place = half * 4 + head
                scaled = both[:, one * HEAD : (one + 1) * HEAD] * inv_ref[:, place : place + 1]
                dmix_ref[half, :, cols] = scaled.astype(BF)
                total = jnp.sum(
                    scaled * mixed_ref[half, :, cols].astype(F32), axis=-1, keepdims=True
                )
                dots = jnp.where(lane == place, total, dots)
    dot_ref[...] = dots

    @pl.when(step == pl.num_programs(0) - 1)
    def _():
        gup_ref[...] = acc_up[...].astype(BF)
        gout_ref[...] = acc_out[...].astype(BF)


def attend_back_kernel(
    normed_ref,
    own_ref,
    other_ref,
    probs_ref,
    dmix_ref,
    dot_ref,
    dheads_ref,
    gin_ref,
    vec_ref,
    acc,
    joined,
    dots_now,
):
    group, step = pl.program_id(0), pl.program_id(1)
    per_group = HALF // HEAD // GROUPS
    width = per_group * HEAD

    @pl.when(step == 0)
    def _():
        acc[...] = jnp.zeros_like(acc)
        vec_ref[...] = jnp.zeros_like(vec_ref)

    @pl.when(group == 0)
    def _():
        for place in range(4):
            lane = (place // 2) * 4 + place % 2
            dots_now[:, place : place + 1] = dot_ref[:, lane : lane + 1]

    @pl.when(group == 1)
    def _():
        for place in range(4):
            lane = (place // 2) * 4 + 2 + place % 2
            dots_now[:, place : place + 1] = dot_ref[:, lane : lane + 1]

    for half, heads_ref in enumerate((own_ref, other_ref)):
        for head in range(per_group):
            cols = slice(head * HEAD, (head + 1) * HEAD)
            place = half * per_group + head
            probs = probs_ref[half, head]
            upstream = dmix_ref[half, :, cols]
            d_probs = mul(upstream, heads_ref[2, :, cols], NT) - dots_now[:, place : place + 1]
            d_scores = (probs.astype(F32) * d_probs).astype(BF)
            d_query = (mul(d_scores, heads_ref[1, :, cols], NN) * SCALE).astype(BF)
            d_keys = (mul(heads_ref[0, :, cols], d_scores, TN) * SCALE).T.astype(BF)
            d_values = mul(probs, upstream, TN).astype(BF)
            for which, value in enumerate((d_query, d_keys, d_values)):
                dheads_ref[half, which, :, cols] = value
                first = half * 3 * width + which * width + head * HEAD
                joined[:, first : first + HEAD] = value
    vec_ref[0:1, :] += column_sum(joined[...].astype(F32))
    for chunk in range(4):
        rows = slice(chunk * 256, (chunk + 1) * 256)
        acc[rows, :] += mul(normed_ref[:, rows], joined[...], TN)

    @pl.when(step == pl.num_programs(1) - 1)
    def _():
        for half in range(2):
            cols = slice(half * 3 * width, (half + 1) * 3 * width)
            gin_ref[half] = acc[:, cols].astype(BF)


def last_kernel(
    x_ref,
    dheads_ref,
    dmid_ref,
    w_own,
    w_other,
    gain_ref,
    grad_ref,
    vec_ref,
    wide,
):
    step = pl.program_id(0)

    @pl.when(step == 0)
    def _():
        vec_ref[...] = jnp.zeros_like(vec_ref)

    for chunk in range(4):
        rows = slice(chunk * 256, (chunk + 1) * 256)
        total = None
        for half, weight in enumerate((w_own, w_other)):
            for which in range(3):
                term = mul(dheads_ref[half, which], weight[which, rows, :], NT)
                total = term if total is None else total + term
        wide[:, rows] = total
    unit, inverse = unit_of(x_ref[...].astype(F32))
    upstream = wide[...]
    vec_ref[0:1, :] += column_sum(upstream * unit)
    vec_ref[1:2, :] += column_sum(upstream)
    grad_ref[...] = dmid_ref[...].astype(F32) + norm_back(upstream, unit, inverse, gain_ref[...])


def reduce_kernel(jobs, *refs):
    count = len(jobs)
    sources, results = refs[:count], refs[count : 2 * count]
    scratch = refs[2 * count : -1]
    own_sem = refs[-1]
    greet(reduction_partners())
    for n, job in enumerate(jobs):
        mine = scratch[6 * n : 6 * n + 6]
        copy = pltpu.make_async_copy(sources[n].at[0], mine[0], own_sem.at[n])
        copy.start()
        copy.wait()
        for tick in range(job.ticks):
            job.tick(mine, tick, sources[n].at[1])
        out = pltpu.make_async_copy(mine[1], results[n], own_sem.at[n])
        out.start()
        out.wait()


def params(**more):
    return pltpu.CompilerParams(vmem_limit_bytes=VMEM_LIMIT, **more)


def per_device(
    latents,
    first_scale,
    first_shift,
    input_weights,
    input_bias,
    output_weight,
    output_bias,
    second_scale,
    second_shift,
    up_weight,
    up_bias,
    down_weight,
    down_bias,
    output_grad,
):
    rows = latents.shape[0]
    images = rows // LAT
    dp, mp = lax.axis_size("dp"), lax.axis_size("mp")
    direct = dp == 16 and mp == 2
    factor = LAT / (rows * dp * mp)
    row = lambda v: v[None, :]
    first_scale, first_shift = row(first_scale), row(first_shift)
    second_scale, second_shift = row(second_scale), row(second_shift)
    output_bias, down_bias = row(output_bias), row(down_bias)

    if direct:
        own = (input_weights, output_weight, up_weight, down_weight)
        small = jnp.concatenate(
            [input_bias, up_bias[None], jnp.zeros((13, HALF), BF)], axis=0
        )
    else:
        gather = lambda v, axis: lax.all_gather(v, "mp", axis=axis, tiled=True)
        w_in, w_out = gather(input_weights, 2), gather(output_weight, 0)
        w_up, w_down = gather(up_weight, 1), gather(down_weight, 0)
        small = jnp.concatenate([gather(input_bias, 1), gather(up_bias, 0)[None]], axis=0)
        own = (w_in[..., :HALF], w_out[:HALF], w_up[:, :HALF], w_down[:HALF])
        others = (w_in[..., HALF:], w_out[HALF:], w_up[:, HALF:], w_down[HALF:], small[:, HALF:])
        small = small[:, :HALF]

    w_shapes = [(3, D, HALF), (HALF, D), (D, HALF), (HALF, D), (16, HALF)]
    normed_shape = shape_of((rows, D), BF)
    heads_shape = shape_of((3, rows, HALF), BF)
    heads_spec = pl.BlockSpec((3, LAT, HALF), lambda i: (0, i, 0))
    vector = kept_spec((1, D))
    bias_spec = whole_spec(small.shape)
    outs = pl.pallas_call(
        functools.partial(first_kernel, direct),
        grid=(images,),
        name="project_own",
        in_specs=[row_spec(D), vector, vector, bias_spec, whole_spec((3, D, HALF))]
        + ([ANY] * 5 if direct else []),
        out_specs=[row_spec(D), heads_spec] + ([ANY] * 5 if direct else []),
        out_shape=[normed_shape, heads_shape]
        + ([shape_of(s, BF) for s in w_shapes] if direct else []),
        scratch_shapes=[pltpu.SemaphoreType.DMA((5,))] * 2 if direct else [],
        compiler_params=params(collective_id=0, has_side_effects=True) if direct else params(),
        cost_estimate=cost(6 * rows * D * HALF, 12 * rows * D),
    )(
        latents,
        first_scale,
        first_shift,
        small,
        own[0],
        *((own + (small,)) if direct else ()),
    )
    normed_one, heads_own = outs[:2]
    if direct:
        others = outs[2:]
    w_in_other, w_out_other, w_up_other, w_down_other, small_other = others
    w_in_own, w_out_own, w_up_own, w_down_own = own

    half_spec = pl.BlockSpec((2, LAT, HALF), lambda i: (0, i, 0))
    half_shape = shape_of((2, rows, HALF), BF)
    head_count = HALF // HEAD
    probs_shape = shape_of((2, head_count, rows, LAT), BF)
    probs_spec = pl.BlockSpec((2, head_count, LAT, LAT), lambda i: (0, 0, i, 0))
    square = (HALF, D)
    tall = (D, HALF)
    (
        block_output,
        heads_other,
        probs,
        inverses,
        mixed,
        middle,
        slope,
        g_down,
        g_sum,
    ) = pl.pallas_call(
        forward_kernel,
        grid=(images,),
        name="forward",
        in_specs=[
            row_spec(D),
            row_spec(D),
            heads_spec,
            row_spec(D),
            whole_spec((3, D, HALF)),
            whole_spec(small_other.shape),
            whole_spec(square),
            whole_spec(square),
            vector,
            vector,
            vector,
            whole_spec(tall),
            whole_spec(tall),
            kept_spec((1, HALF)),
            kept_spec((1, HALF)),
            whole_spec(square),
            whole_spec(square),
            vector,
        ],
        out_specs=[
            row_spec(D),
            heads_spec,
            probs_spec,
            row_spec(HEAD),
            half_spec,
            row_spec(D),
            half_spec,
            kept_spec((2, HALF, D)),
            kept_spec((8, D)),
        ],
        out_shape=[
            shape_of((rows, D), F32),
            heads_shape,
            probs_shape,
            shape_of((rows, HEAD), F32),
            half_shape,
            shape_of((rows, D), BF),
            half_shape,
            shape_of((2, HALF, D), BF),
            shape_of((8, D), F32),
        ],
        scratch_shapes=[
            pltpu.VMEM((2, HALF, D), F32),
            pltpu.VMEM((LAT, D), BF),
            pltpu.VMEM((2, LAT, HALF), BF),
            pltpu.VMEM((LAT, D), F32),
        ],
        compiler_params=params(),
        cost_estimate=cost(16 * rows * D * D, 24 * rows * D),
    )(
        latents,
        normed_one,
        heads_own,
        output_grad,
        w_in_other,
        small_other,
        w_out_own,
        w_out_other,
        output_bias,
        second_scale,
        second_shift,
        w_up_own,
        w_up_other,
        small[2:3],
        small_other[2:3],
        w_down_own,
        w_down_other,
        down_bias,
    )

    d_middle, d_mixed, d_dots, g_up, g_out, vec_two, vec_up = pl.pallas_call(
        feed_back_kernel,
        grid=(images,),
        name="feed_back",
        in_specs=[
            row_spec(D),
            half_spec,
            row_spec(D),
            half_spec,
            row_spec(HEAD),
            whole_spec(square),
            whole_spec(square),
            whole_spec(tall),
            whole_spec(tall),
            whole_spec(square),
            whole_spec(square),
            vector,
            vector,
        ],
        out_specs=[
            row_spec(D),
            half_spec,
            row_spec(HEAD),
            kept_spec((2, HALF, D)),
            kept_spec((2, HALF, D)),
            kept_spec((8, D)),
            kept_spec((8, HALF)),
        ],
        out_shape=[
            shape_of((rows, D), BF),
            half_shape,
            shape_of((rows, HEAD), F32),
            shape_of((2, HALF, D), BF),
            shape_of((2, HALF, D), BF),
            shape_of((8, D), F32),
            shape_of((8, HALF), F32),
        ],
        scratch_shapes=[
            pltpu.VMEM((2, HALF, D), F32),
            pltpu.VMEM((2, HALF, D), F32),
            pltpu.VMEM((LAT, D), BF),
            pltpu.VMEM((LAT, D), F32),
            pltpu.VMEM((2, LAT, HALF), BF),
            pltpu.VMEM((LAT, D), F32),
        ],
        compiler_params=params(),
        cost_estimate=cost(10 * rows * D * D, 14 * rows * D),
    )(
        output_grad,
        slope,
        middle,
        mixed,
        inverses,
        w_down_own,
        w_down_other,
        w_up_own,
        w_up_other,
        w_out_own,
        w_out_other,
        second_scale,
        second_shift,
    )

    per_group = head_count // GROUPS
    width = per_group * HEAD
    group_heads = pl.BlockSpec((3, LAT, width), lambda g, i: (0, i, g))
    d_heads, g_in, vec_in = pl.pallas_call(
        attend_back_kernel,
        grid=(GROUPS, images),
        name="attend_back",
        in_specs=[
            pl.BlockSpec((LAT, D), lambda g, i: (i, 0)),
            group_heads,
            group_heads,
            pl.BlockSpec((2, per_group, LAT, LAT), lambda g, i: (0, g, i, 0)),
            pl.BlockSpec((2, LAT, width), lambda g, i: (0, i, g)),
            pl.BlockSpec((LAT, HEAD), lambda g, i: (i, 0)),
        ],
        out_specs=[
            pl.BlockSpec((2, 3, LAT, width), lambda g, i: (0, 0, i, g)),
            pl.BlockSpec((None, 2, D, 3 * width), lambda g, i: (g, 0, 0, 0)),
            pl.BlockSpec((None, 8, 6 * width), lambda g, i: (g, 0, 0)),
        ],
        out_shape=[
            shape_of((2, 3, rows, HALF), BF),
            shape_of((GROUPS, 2, D, 3 * width), BF),
            shape_of((GROUPS, 8, 6 * width), F32),
        ],
        scratch_shapes=[
            pltpu.VMEM((D, 6 * width), F32),
            pltpu.VMEM((LAT, 6 * width), BF),
            pltpu.VMEM((LAT, HEAD), F32),
        ],
        compiler_params=params(),
        cost_estimate=cost(8 * rows * D * D, 20 * rows * D),
    )(normed_one, heads_own, heads_other, probs, d_mixed, d_dots)

    latents_grad, vec_one = pl.pallas_call(
        last_kernel,
        grid=(images,),
        name="input_back",
        in_specs=[
            row_spec(D),
            pl.BlockSpec((2, 3, LAT, HALF), lambda i: (0, 0, i, 0)),
            row_spec(D),
            whole_spec((3, D, HALF)),
            whole_spec((3, D, HALF)),
            vector,
        ],
        out_specs=[row_spec(D), kept_spec((8, D))],
        out_shape=[shape_of((rows, D), F32), shape_of((8, D), F32)],
        scratch_shapes=[pltpu.VMEM((LAT, D), F32)],
        compiler_params=params(),
        cost_estimate=cost(6 * rows * D * D, 14 * rows * D),
    )(latents, d_heads, d_middle, w_in_own, w_in_other, first_scale)

    g_first_scale, g_first_shift = vec_one[0], vec_one[1]
    g_second_scale, g_second_shift, g_output_bias = vec_two[0], vec_two[1], vec_two[2]
    g_down_bias = g_sum[0]
    by_group = vec_in[:, 0].reshape(GROUPS, 2, 3, width)
    in_bias = jnp.transpose(by_group, (1, 2, 0, 3)).reshape(2, 3, HALF)
    sharded = jnp.stack([in_bias[:, 0], in_bias[:, 2], vec_up[:2]], axis=1)

    if direct:
        me = lax.axis_index("mp")
        sharded = jnp.where(me == 0, sharded, sharded[::-1])
        sharded = jnp.transpose(sharded, (1, 0, 2)).reshape(3, D)
    else:
        sharded = jnp.transpose(sharded, (1, 0, 2)).reshape(3, D)
    vectors = lax.psum(
        jnp.concatenate(
            [
                jnp.stack(
                    [
                        g_first_scale,
                        g_first_shift,
                        g_output_bias,
                        g_second_scale,
                        g_second_shift,
                        g_down_bias,
                    ]
                ),
                sharded,
            ]
        ),
        ("dp", "mp"),
    )
    vectors = vectors * factor
    own_width = D // mp
    mine = lax.dynamic_slice_in_dim(vectors[6:], lax.axis_index("mp") * own_width, own_width, 1)

    if direct:
        parts = ((0, 384), (384, 768), (768, 1024))
        jobs = [
            Reduction(HALF, D, parts, ORDERS),
            Reduction(HALF, D, parts, ORDERS),
            Reduction(HALF, D, parts, ORDERS),
        ] + [
            Reduction(D, 3 * width, ((0, width), (width, 2 * width), (2 * width, 3 * width)), ORDERS)
        ] * GROUPS
        sources = [g_down, g_up, g_out] + [g_in[g] for g in range(GROUPS)]
        g_down, g_up, g_out, *g_in = pl.pallas_call(
            functools.partial(reduce_kernel, jobs),
            name="reduce",
            in_specs=[ANY] * len(jobs),
            out_specs=[ANY] * len(jobs),
            out_shape=[shape_of((job.rows, job.columns), BF) for job in jobs],
            scratch_shapes=sum([job.scratch() for job in jobs], [])
            + [pltpu.SemaphoreType.DMA((len(jobs),))],
            compiler_params=params(collective_id=1, has_side_effects=True),
        )(*sources)
        g_up = g_up.T
        g_in = jnp.stack([part.reshape(D, 3, width) for part in g_in], axis=2)
        g_in = jnp.transpose(g_in, (1, 0, 2, 3)).reshape(3, D, HALF)
    else:
        g_down, g_up, g_out = (v.reshape(D, D) for v in (g_down, g_up, g_out))
        g_in = jnp.transpose(g_in.reshape(GROUPS, 2, D, 3, width), (3, 2, 1, 0, 4))
        g_in = g_in.reshape(3, D, D)
        scatter = lambda v, axis: lax.psum(
            lax.psum_scatter(v, "mp", scatter_dimension=axis, tiled=True), "dp"
        )
        g_down, g_up, g_out = scatter(g_down, 0), scatter(g_up.T, 1), scatter(g_out, 0)
        g_in = scatter(g_in, 2)

    final = lambda v: v.astype(F32) * factor
    return (
        block_output,
        latents_grad,
        vectors[0],
        vectors[1],
        final(g_in),
        mine[:2],
        final(g_out),
        vectors[2],
        vectors[3],
        vectors[4],
        final(g_up),
        mine[2],
        final(g_down),
        vectors[5],
    )


def solution(mesh):
    return jax.shard_map(
        per_device,
        mesh=mesh,
        in_specs=(
            P(("dp", "mp"), None),
            P(),
            P(),
            P(None, None, "mp"),
            P(None, "mp"),
            P("mp", None),
            P(),
            P(),
            P(),
            P(None, "mp"),
            P("mp"),
            P("mp", None),
            P(),
            P(("dp", "mp"), None),
        ),
        out_specs=(
            P(("dp", "mp"), None),
            P(("dp", "mp"), None),
            P(),
            P(),
            P(None, None, "mp"),
            P(None, "mp"),
            P("mp", None),
            P(),
            P(),
            P(),
            P(None, "mp"),
            P("mp"),
            P("mp", None),
            P(),
        ),
        check_vma=False,
    )
```

time: 1270 us -> 618 us (0.49)
  Pallas kernels: 0 us -> 527 us
  matrix products: 411 us -> 0 us
  waiting for transfers between devices: 302 us -> 0 us
  local copies, waits for them, and re-layouts: 246 us -> 30 us
  other arithmetic: 190 us -> 8.21 us
  blocking collectives: 84.6 us -> 42.1 us
  between operations: 14.5 us -> 1.25 us
    pallas_call x0 -> x6, Pallas kernels: none -> 527 us  [the longest x1 227 us: per_device(): pl.pallas_call(functools.partial(reduce_kernel, jobs), name='reduce', in_...]
    dot_general x124 -> x0, matrix products: 411 us -> none  [the longest x1 35.1 us: per_device(): jnp.einsum('nd,cde->cne', rows_one, input_weights, preferred_element_type...]
    psum x1 -> x0, waiting for transfers between devices: 130 us -> none  [per_device(): lax.psum(g_input_weights.astype(jnp.bfloat16), 'dp').astype(jnp.float32)]
    reduce_scatter x4 -> x0, waiting for transfers between devices: 94.3 us -> none  [the longest x1 46.3 us: per_device(): lax.psum_scatter(jnp.dot(mixed_heads, output_weight, preferred_element_ty...]
    reduce_sum x24 -> x0, other arithmetic: 93.7 us -> none  [the longest x1 28.1 us: per_device(): g_output_bias = jnp.sum(d_middle, axis=0)]
    all_gather x4 -> x0, waiting for transfers between devices: 77.2 us -> none  [the longest x1 32.2 us: per_device(): rows_one = lax.all_gather(normed_one, 'mp', axis=0, tiled=True)]
    dynamic_slice x48 -> x0, local copies, waits for them, and re-layouts: 71.9 us -> none  [the longest x32 62.6 us: one_image(): lax.dynamic_slice_in_dim(d_mixed, image_index * LAT, LAT, 0)]
    dynamic_update_slice x32 -> x0, local copies, waits for them, and re-layouts: 62.9 us -> none  [attend(): lax.map(one_image, jnp.arange(image_count, dtype=jnp.int32))]
  transfers between devices with their start and end apart: 9 -> 0, of which waited for: 8 -> 0; matrix products, arithmetic and copies ran while one was open for 12% -> 0% of each run, Pallas kernels for 0% -> 0%
where the time goes in v1:
time: 618 us; the launch traced here: 608 us
  Pallas kernels  527 us (85%)
  blocking collectives  42.1 us (7%)
  local copies, waits for them, and re-layouts  30 us (5%)
  other arithmetic  8.21 us (1%)
    pallas_call x1, Pallas kernels, per_device(): pl.pallas_call(functools.partial(reduce_kernel, jobs), name='reduce', in_...  227 us
    pallas_call x1, Pallas kernels, per_device(): pl.pallas_call(forward_kernel, grid=(images,), name='forward', in_specs=[...  95.4 us
    pallas_call x1, Pallas kernels, per_device(): pl.pallas_call(attend_back_kernel, grid=(GROUPS, images), name='attend_ba...  75.7 us
    pallas_call x1, Pallas kernels, per_device(): pl.pallas_call(feed_back_kernel, grid=(images,), name='feed_back', in_spe...  65 us
    psum x1, blocking collectives, per_device(): lax.psum(jnp.concatenate([jnp.stack([g_first_scale, g_first_shift, g_outp...  42.1 us
    pallas_call x1, Pallas kernels, per_device(): pl.pallas_call(last_kernel, grid=(images,), name='input_back', in_specs=[...  40.5 us
    pallas_call x1, Pallas kernels, per_device(): pl.pallas_call(functools.partial(first_kernel, direct), grid=(images,), n...  22.8 us

profile of v1, /device:TPU:0, one launch (start us, length us, event | category | flops | bytes accessed | tf_op | source)
XLA Modules:
  0.0 608.4 jit_solution(6509651399642995426)
XLA Ops:
  0.7 0.1 pad.7.clone
  0.7 0.7 broadcast_in_dim.26.ub_own
  1.4 1.4 maximum_maximum_fusion.bias_ref.refs_4_
  2.8 22.8 %project_own.1 = (bf16[4096,1024]{1,0:T(8,128)(2,1)}, bf16[3,4096,512]{2,1,0:T(8,128)(2,1)}, bf16[3,1024,512]{2,1,0:T(8,128)(2,1)}, bf16[512,1024]{1,0:T(8,128)(...) custom-call(bf16[4096,1024]{1,0:T(8,128)(2,1)} %x_ref.5, f32[1,1024]{1,0:T(1,128)} %bitcast.52, ...), custom_call_target="tpu_custom_call" | custom-call | flops 12884901888 | bytes 50331648 | tf_op jit(solution)/shard_map/project_own/pallas_call | solution.py:596
  25.6 1.3 slice.64.ub_other
  26.9 95.4 %forward.1 = (f32[4096,1024]{1,0:T(8,128)}, bf16[3,4096,512]{2,1,0:T(8,128)(2,1)}, bf16[2,4,4096,512]{3,2,1,0:T(8,128)(2,1)}, f32[4096,128]{1,0:T(8,128)}, bf16[...) custom-call(bf16[4096,1024]{1,0:T(8,128)(2,1)} %x_ref.5, ...), custom_call_target="tpu_custom_call" | custom-call | flops 68719476736 | bytes 100663296 | tf_op jit(solution)/shard_map/forward/pallas_call | solution.py:639
  122.3 0.8 slice.68
  123.1 65.0 %feed_back.1 = (bf16[4096,1024]{1,0:T(8,128)(2,1)}, bf16[2,4096,512]{2,1,0:T(8,128)(2,1)}, f32[4096,128]{1,0:T(8,128)}, bf16[2,512,1024]{2,1,0:T(8,128)(2,1)}, b...) custom-call(bf16[4096,1024]{1,0:T(8,128)(2,1)} %g_ref.3, ...), custom_call_target="tpu_custom_call" | custom-call | flops 42949672960 | bytes 58720256 | tf_op jit(solution)/shard_map/feed_back/pallas_call | solution.py:714
  188.1 75.7 %attend_back.1 = (bf16[2,3,4096,512]{3,2,1,0:T(8,128)(2,1)}, bf16[2,2,1024,768]{3,2,1,0:T(8,128)(2,1)}, f32[2,8,1536]{2,1,0:T(8,128)}) custom-call(bf16[4096,1024]{1,0:T(8,128)(2,1)} %get-tuple-element.47.normed_ref, bf16[3,4096,512]{2,1,0:T(8,128)(2,1)} %get-tuple-element.48.own_ref, bf16[3,4096,512]{2,1,0:T(8,128)(2,1)} %get-tuple-element.55.other_ref, ...), custom_call_target="tpu_custom_call" | custom-call | flops 34359738368 | bytes 83886080 | tf_op jit(solution)/shard_map/attend_back/pallas_call | solution.py:780
  263.8 40.5 %input_back.1 = (f32[4096,1024]{1,0:T(8,128)}, f32[8,1024]{1,0:T(8,128)}) custom-call(bf16[4096,1024]{1,0:T(8,128)(2,1)} %x_ref.5, bf16[2,3,4096,512]{3,2,1,0:T(8,128)(2,1)} %get-tuple-element.63.dheads_ref, bf16[4096,1024]{1,0:T(8,128)(2,1)} %get-tuple-element.64.dmid_ref, bf16[3,1024,512]{2,1,0:T(8,128)(2,1)} %w_own.1, ...), custom_call_target="tpu_custom_call" | custom-call | flops 25769803776 | bytes 58720256 | tf_op jit(solution)/shard_map/input_back/pallas_call | solution.py:811
  304.3 0.7 slice_bitcast_fusion.2
  305.0 0.8 slice.66
  305.8 0.8 slice.67
  306.5 0.8 slice.65
  307.3 0.9 slice_reduce_fusion
  308.3 0.2 rev.3
  308.5 0.2 concatenate.8
  308.7 42.1 %psum.7 = f32[9,1024]{1,0:T(8,128)S(1)} all-reduce(f32[9,1024]{1,0:T(8,128)S(1)} %concatenate.8), channel_id=1, replica_groups=mesh['dp'=16,'mp'=2] {'dp','mp'}, use_global_device_ids=true, to_apply=%region_0.1 | all-reduce | flops 9216 | bytes 73728 | tf_op jit(solution)/shard_map/psum | solution.py:843
  350.8 0.6 fusion
  351.5 0.7 dynamic-slice.1
  352.1 0.6 constant_dynamic-slice_fusion
  352.7 5.9 slice_bitcast_fusion
  358.6 227.3 %reduce.3 = (bf16[512,1024]{1,0:T(8,128)(2,1)}, bf16[512,1024]{1,0:T(8,128)(2,1)}, bf16[512,1024]{1,0:T(8,128)(2,1)}, bf16[1024,768]{1,0:T(8,128)(2,1)}, bf16[1024,768]{1,0:T(8,128)(2,1)}) custom-call(bf16[2,512,1024]{2,1,0:T(8,128)(2,1)} %get-tuple-element.71.refs_0_, bf16[2,512,1024]{2,1,0:T(8,128)(2,1)} %get-tuple-element.72.refs_1_, ...), custom_call_target="tpu_custom_call" | custom-call | tf_op jit(solution)/shard_map/reduce/pallas_call | solution.py:875
  586.0 1.7 copy.36
  587.7 1.7 copy.37
  589.4 2.8 convert_multiply_fusion.1
  592.2 0.9 multiply_bitcast_fusion
  593.1 3.2 copy.38
  596.4 6.6 %copy.39 = f32[3,1024,512]{2,1,0:T(8,128)} copy(f32[3,1024,512]{1,2,0:T(8,128)} %bitcast.33) | data formatting | bytes 12582912
  603.0 0.0 copy-done
  603.0 3.1 convert_multiply_fusion
  606.1 1.8 copy.40
  (13 shorter events, 0.1 us)
Async XLA Ops:
  1.4 24.2 %copy-start.1 = (bf16[1,512]{1,0:T(2,128)(2,1)}, bf16[1,512]{1,0:T(2,128)(2,1)S(1)}, u32[]{:S(2)}) copy-start(bf16[1,512]{1,0:T(2,128)(2,1)S(1)} %broadcast_in_dim.26.ub_own) | copy-start | bytes 3076
  596.4 6.7 %copy-start = (bf16[512,1024]{1,0:T(8,128)(2,1)S(1)}, bf16[512,1024]{1,0:T(8,128)(2,1)}, u32[]{:S(2)}) copy-start(bf16[512,1024]{1,0:T(8,128)(2,1)} %get-tuple-element.79) | copy-start | bytes 3145732

commit v2 on v1

--- a/solution.py
+++ b/solution.py
@@ -48,7 +48,7 @@
 
 
 def column_sum(values):
-    return jnp.sum(values, axis=0, keepdims=True)
+    return jnp.sum(values.reshape(values.shape[0] // 8, 8, values.shape[1]), axis=0)
 
 
 def row_spec(width):
@@ -118,6 +118,7 @@
             pltpu.SemaphoreType.DMA((2,)),
             pltpu.SemaphoreType.DMA((len(self.parts), stages)),
             pltpu.SemaphoreType.DMA((len(self.parts), stages)),
+            pltpu.SemaphoreType.DMA((2,)),
         ]
 
     def offset(self, part, level):
@@ -136,7 +137,7 @@
         return pl.ds(first, last - first)
 
     def halving(self, refs, part, stage):
-        cur, _, recv, _, send_sem, recv_sem = refs
+        cur, _, recv, _, send_sem, recv_sem = refs[:6]
         size = self.rows >> (stage + 1)
         bit = self.orders[part][stage]
         on = lax.rem(lax.axis_index("dp") // (1 << bit), 2)
@@ -153,7 +154,7 @@
         return copy, self.aligned(base + on * size, size), pl.ds(landing, size), cols
 
     def doubling(self, refs, part, step):
-        _, full, _, _, send_sem, recv_sem = refs
+        _, full, _, _, send_sem, recv_sem = refs[:6]
         stage = self.bits - 1 - step
         size = self.rows >> (stage + 1)
         rows = self.aligned(self.offset(part, stage + 1), size)
@@ -200,7 +201,55 @@
                 self.doubling(refs, part, step + 1).start()
 
 
+class Task:
+    def __init__(self, job, refs, source, result, places, staged=False):
+        self.job, self.refs, self.source, self.result = job, refs, source, result
+        self.places, self.staged = places, staged
+
+    def load(self):
+        return pltpu.make_async_copy(self.source.at[0], self.refs[0], self.refs[6].at[0])
+
+    def store(self):
+        return pltpu.make_async_copy(self.refs[1], self.result, self.refs[6].at[1])
+
+    def run(self, tick):
+        if tick == 0 and not self.staged:
+            self.load().start()
+        if tick == 1 and not self.staged:
+            self.load().wait()
+        self.job.tick(self.refs, tick, self.source if self.staged else self.source.at[1])
+        if tick == self.job.ticks - 1:
+            self.store().start()
+
+    def finish(self):
+        self.store().wait()
+
+
+def run_tasks(step, place, tasks):
+    for now in sorted({at[0] for task in tasks for at in task.places if at[1] == place}):
+
+        @pl.when(step == now)
+        def _():
+            for task in tasks:
+                for tick, at in enumerate(task.places):
+                    if at == (now, place):
+                        task.run(tick)
+
+
 ORDERS = ((0, 1, 2, 3), (1, 2, 3, 0), (2, 3, 0, 1))
+
+
+def halves(*numbers):
+    return tuple((n // 2, n % 2) for n in numbers)
+
+
+FEED_PLACES = halves(0, 1, 2, 3, 4, 5, 6, 7, 8, 10)
+ATTEND_PLACES = (
+    halves(0, 1, 3, 5, 6, 7, 8, 9, 11, 13),
+    halves(2, 3, 6, 8, 9, 10, 11, 12, 14, 16),
+    ((7, 2),) + halves(17, 20, 22, 24, 25, 26, 28, 30) + ((15, 2),),
+)
+LAST_PLACES = halves(0, 1, 4, 6, 8, 9, 10, 12, 14) + ((7, 2),)
 
 
 def reduction_partners():
@@ -342,7 +391,7 @@
         )
     for half in range(2):
         acc[half] += mul(act[half], g_ref[...], TN)
-    gsum_ref[0:1, :] += column_sum(g_ref[...].astype(F32))
+    gsum_ref[...] += column_sum(g_ref[...].astype(F32))
 
     @pl.when(step == pl.num_programs(0) - 1)
     def _():
@@ -350,6 +399,8 @@
 
 
 def feed_back_kernel(
+    job,
+    places,
     g_ref,
     slope_ref,
     middle_ref,
@@ -363,35 +414,36 @@
     wo_other,
     gain_ref,
     shift_ref,
-    dmid_ref,
-    dmix_ref,
-    dot_ref,
-    gup_ref,
-    gout_ref,
-    vec_ref,
-    ubias_ref,
-    acc_up,
-    acc_out,
-    normed_two,
-    unit_ref,
-    dhid,
-    wide,
+    *refs,
 ):
+    tasks = []
+    if job is not None:
+        source, refs = refs[0], refs[1:]
+    outs, refs = refs[:7], refs[7:]
+    if job is not None:
+        result, refs = refs[0], refs[1:]
+    dmid_ref, dmix_ref, dot_ref, gup_ref, gout_ref, vec_ref, ubias_ref = outs
+    acc_up, acc_out, normed_two, unit_ref, dhid, wide = refs[:6]
+    if job is not None:
+        tasks.append(Task(job, refs[6:], source, result, places))
     step = pl.program_id(0)
 
     @pl.when(step == 0)
     def _():
+        if tasks:
+            greet(reduction_partners())
         acc_up[...] = jnp.zeros_like(acc_up)
         acc_out[...] = jnp.zeros_like(acc_out)
         vec_ref[...] = jnp.zeros_like(vec_ref)
         ubias_ref[...] = jnp.zeros_like(ubias_ref)
 
+    run_tasks(step, 0, tasks)
     for half, weight in enumerate((wd_own, wd_other)):
         for chunk in range(2):
             cols = slice(chunk * 256, (chunk + 1) * 256)
             down = mul(g_ref[...], weight[cols, :], NT)
             dhid[half, :, cols] = (down * slope_ref[half, :, cols].astype(F32)).astype(BF)
-        ubias_ref[half : half + 1, :] += column_sum(dhid[half].astype(F32))
+        ubias_ref[half] += column_sum(dhid[half].astype(F32))
     unit, inverse = unit_of(middle_ref[...].astype(F32))
     unit_ref[...] = unit
     normed_two[...] = (unit * gain_ref[...] + shift_ref[...]).astype(BF)
@@ -400,12 +452,13 @@
     for chunk in range(4):
         rows = slice(chunk * 256, (chunk + 1) * 256)
         wide[:, rows] = mul(dhid[0], wu_own[rows, :], NT) + mul(dhid[1], wu_other[rows, :], NT)
+    run_tasks(step, 1, tasks)
     upstream = wide[...]
     unit = unit_ref[...]
-    vec_ref[0:1, :] += column_sum(upstream * unit)
-    vec_ref[1:2, :] += column_sum(upstream)
+    vec_ref[0] += column_sum(upstream * unit)
+    vec_ref[1] += column_sum(upstream)
     dmid = g_ref[...].astype(F32) + norm_back(upstream, unit, inverse, gain_ref[...])
-    vec_ref[2:3, :] += column_sum(dmid)
+    vec_ref[2] += column_sum(dmid)
     dmid_ref[...] = dmid.astype(BF)
     lane = lax.broadcasted_iota(jnp.int32, (LAT, HEAD), 1)
     dots = jnp.zeros((LAT, HEAD), F32)
@@ -429,25 +482,45 @@
     def _():
         gup_ref[...] = acc_up[...].astype(BF)
         gout_ref[...] = acc_out[...].astype(BF)
+        for task in tasks:
+            task.finish()
 
 
 def attend_back_kernel(
+    jobs,
+    places,
     normed_ref,
     own_ref,
     other_ref,
     probs_ref,
     dmix_ref,
     dot_ref,
-    dheads_ref,
-    gin_ref,
-    vec_ref,
-    acc,
-    joined,
-    dots_now,
+    *refs,
 ):
+    tasks, count = [], len(jobs)
+    if jobs:
+        sources, refs = refs[: count - 1], refs[count - 1 :]
+    dheads_ref, gin_ref, vec_ref = refs[:3]
+    refs = refs[3:]
+    if jobs:
+        results, refs = refs[:count], refs[count:]
+    acc, joined, dots_now = refs[:3]
+    if jobs:
+        staged, refs = refs[3], refs[4:]
+        for n, job in enumerate(jobs):
+            mine = refs[7 * n : 7 * n + 7]
+            last = n == count - 1
+            tasks.append(Task(job, mine, staged if last else sources[n], results[n], places[n], last))
     group, step = pl.program_id(0), pl.program_id(1)
+    now = group * pl.num_programs(1) + step
     per_group = HALF // HEAD // GROUPS
     width = per_group * HEAD
+
+    if tasks:
+
+        @pl.when(now == 0)
+        def _():
+            greet(reduction_partners())
 
     @pl.when(step == 0)
     def _():
@@ -466,6 +539,7 @@
             lane = (place // 2) * 4 + 2 + place % 2
             dots_now[:, place : place + 1] = dot_ref[:, lane : lane + 1]
 
+    run_tasks(now, 0, tasks)
     for half, heads_ref in enumerate((own_ref, other_ref)):
         for head in range(per_group):
             cols = slice(head * HEAD, (head + 1) * HEAD)
@@ -481,35 +555,107 @@
                 dheads_ref[half, which, :, cols] = value
                 first = half * 3 * width + which * width + head * HEAD
                 joined[:, first : first + HEAD] = value
-    vec_ref[0:1, :] += column_sum(joined[...].astype(F32))
+            if half == 1 and head == per_group - 1:
+                run_tasks(now, 1, tasks)
+    vec_ref[...] += column_sum(joined[...].astype(F32))
     for chunk in range(4):
         rows = slice(chunk * 256, (chunk + 1) * 256)
         acc[rows, :] += mul(normed_ref[:, rows], joined[...], TN)
 
-    @pl.when(step == pl.num_programs(1) - 1)
+    @pl.when((now if tasks else step) == pl.num_programs(1) * (GROUPS if tasks else 1) - 1)
     def _():
         for half in range(2):
             cols = slice(half * 3 * width, (half + 1) * 3 * width)
             gin_ref[half] = acc[:, cols].astype(BF)
 
+    if tasks:
+
+        @pl.when(now == pl.num_programs(1) - 1)
+        def _():
+            tasks[-1].refs[0][...] = acc[:, : 3 * width].astype(BF)
+            staged[...] = acc[:, 3 * width :].astype(BF)
+
+    run_tasks(now, 2, tasks)
+
+    if tasks:
+
+        @pl.when(now == pl.num_programs(0) * pl.num_programs(1) - 1)
+        def _():
+            for task in tasks:
+                task.finish()
+
+
+def pack_vectors(vec_ref, two_ref, sum_ref, up_ref, in_ref, out_ref):
+    total = lambda v: jnp.sum(v, axis=0, keepdims=True)
+    width = HALF // GROUPS
+    out_ref[...] = jnp.zeros_like(out_ref)
+    out_ref[0:1, :] = total(vec_ref[0])
+    out_ref[1:2, :] = total(vec_ref[1])
+    out_ref[2:3, :] = total(two_ref[2])
+    out_ref[3:4, :] = total(two_ref[0])
+    out_ref[4:5, :] = total(two_ref[1])
+    out_ref[5:6, :] = total(sum_ref[...])
+    for half in range(2):
+        for group in range(GROUPS):
+            cols = slice(half * HALF + group * width, half * HALF + (group + 1) * width)
+            for row, which in ((6, 0), (7, 2)):
+                first = (half * 3 + which) * width
+                out_ref[row : row + 1, cols] = total(in_ref[group, :, first : first + width])
+        out_ref[8:9, half * HALF : (half + 1) * HALF] = total(up_ref[half])
+
+
+def sum_vectors(held, landed, send_sem, recv_sem):
+    partners = reduction_partners()
+    for stage, partner in enumerate(partners):
+        copy = remote(
+            held.at[stage], landed.at[stage], send_sem.at[stage], recv_sem.at[stage], partner
+        )
+        copy.start()
+        copy.wait()
+        got = landed[stage]
+        if stage == 0:
+            crossed = jnp.concatenate([got[:, HALF:], got[:, :HALF]], axis=1)
+            row = lax.broadcasted_iota(jnp.int32, got.shape, 0)
+            got = jnp.where(row < 6, got, crossed)
+        held[stage + 1] = held[stage] + got
+
 
 def last_kernel(
+    job,
+    places,
+    factor,
     x_ref,
     dheads_ref,
     dmid_ref,
     w_own,
     w_other,
     gain_ref,
-    grad_ref,
-    vec_ref,
-    wide,
+    two_ref,
+    sum_ref,
+    up_ref,
+    in_ref,
+    *refs,
 ):
+    tasks = []
+    if job is not None:
+        source, refs = refs[0], refs[1:]
+    (grad_ref, total_ref), refs = refs[:2], refs[2:]
+    if job is not None:
+        result, refs = refs[0], refs[1:]
+    (wide, vec_ref), refs = refs[:2], refs[2:]
+    if job is not None:
+        vectors, refs = refs[:4], refs[4:]
+        tasks.append(Task(job, refs, source, result, places))
     step = pl.program_id(0)
+    last = pl.num_programs(0) - 1
 
     @pl.when(step == 0)
     def _():
+        if tasks:
+            greet(reduction_partners())
         vec_ref[...] = jnp.zeros_like(vec_ref)
 
+    run_tasks(step, 0, tasks)
     for chunk in range(4):
         rows = slice(chunk * 256, (chunk + 1) * 256)
         total = None
@@ -518,29 +664,42 @@
                 term = mul(dheads_ref[half, which], weight[which, rows, :], NT)
                 total = term if total is None else total + term
         wide[:, rows] = total
+    run_tasks(step, 1, tasks)
     unit, inverse = unit_of(x_ref[...].astype(F32))
     upstream = wide[...]
-    vec_ref[0:1, :] += column_sum(upstream * unit)
-    vec_ref[1:2, :] += column_sum(upstream)
-    grad_ref[...] = dmid_ref[...].astype(F32) + norm_back(upstream, unit, inverse, gain_ref[...])
-
-
-def reduce_kernel(jobs, *refs):
-    count = len(jobs)
-    sources, results = refs[:count], refs[count : 2 * count]
-    scratch = refs[2 * count : -1]
-    own_sem = refs[-1]
-    greet(reduction_partners())
-    for n, job in enumerate(jobs):
-        mine = scratch[6 * n : 6 * n + 6]
-        copy = pltpu.make_async_copy(sources[n].at[0], mine[0], own_sem.at[n])
-        copy.start()
-        copy.wait()
-        for tick in range(job.ticks):
-            job.tick(mine, tick, sources[n].at[1])
-        out = pltpu.make_async_copy(mine[1], results[n], own_sem.at[n])
-        out.start()
-        out.wait()
+    vec_ref[0] += column_sum(upstream * unit)
+    vec_ref[1] += column_sum(upstream)
+    grad = dmid_ref[...].astype(F32) + norm_back(upstream, unit, inverse, gain_ref[...])
+    grad_ref[...] = grad.astype(BF)
+    run_tasks(step, 2, tasks)
+
+    @pl.when(step == last)
+    def _():
+        if tasks:
+            pack_vectors(vec_ref, two_ref, sum_ref, up_ref, in_ref, vectors[0].at[0])
+            sum_vectors(*vectors)
+            total_ref[...] = vectors[0][len(reduction_partners())] * factor
+        else:
+            pack_vectors(vec_ref, two_ref, sum_ref, up_ref, in_ref, total_ref)
+        for task in tasks:
+            task.finish()
+
+
+def finish_kernel(factor, lat_ref, *refs):
+    if len(refs) > 1:
+        down_in, up_in, out_in, in_a, in_b, lat_out, down_out, up_out, out_out, in_out = refs
+        width = HALF // GROUPS
+        down_out[...] = down_in[...].astype(F32) * factor
+        out_out[...] = out_in[...].astype(F32) * factor
+        up_out[...] = up_in[...].astype(F32).T * factor
+        for which in range(3):
+            for group, part in enumerate((in_a, in_b)):
+                in_out[which, :, group * width : (group + 1) * width] = (
+                    part[:, which * width : (which + 1) * width].astype(F32) * factor
+                )
+    else:
+        (lat_out,) = refs
+    lat_out[...] = lat_ref[...].astype(F32)
 
 
 def params(**more):
@@ -626,6 +785,9 @@
     probs_spec = pl.BlockSpec((2, head_count, LAT, LAT), lambda i: (0, 0, i, 0))
     square = (HALF, D)
     tall = (D, HALF)
+    parts = ((0, 384), (384, 768), (768, 1024))
+    job = Reduction(HALF, D, parts, ORDERS) if direct else None
+    result = shape_of(square, BF)
     (
         block_output,
         heads_other,
@@ -711,8 +873,8 @@
         down_bias,
     )
 
-    d_middle, d_mixed, d_dots, g_up, g_out, vec_two, vec_up = pl.pallas_call(
-        feed_back_kernel,
+    d_middle, d_mixed, d_dots, g_up, g_out, vec_two, vec_up, *sums = pl.pallas_call(
+        functools.partial(feed_back_kernel, job, FEED_PLACES),
         grid=(images,),
         name="feed_back",
         in_specs=[
@@ -729,25 +891,28 @@
             whole_spec(square),
             vector,
             vector,
-        ],
+        ]
+        + ([ANY] if direct else []),
         out_specs=[
             row_spec(D),
             half_spec,
             row_spec(HEAD),
             kept_spec((2, HALF, D)),
             kept_spec((2, HALF, D)),
-            kept_spec((8, D)),
-            kept_spec((8, HALF)),
-        ],
+            kept_spec((3, 8, D)),
+            kept_spec((2, 8, HALF)),
+        ]
+        + ([ANY] if direct else []),
         out_shape=[
             shape_of((rows, D), BF),
             half_shape,
             shape_of((rows, HEAD), F32),
             shape_of((2, HALF, D), BF),
             shape_of((2, HALF, D), BF),
-            shape_of((8, D), F32),
-            shape_of((8, HALF), F32),
-        ],
+            shape_of((3, 8, D), F32),
+            shape_of((2, 8, HALF), F32),
+        ]
+        + ([result] if direct else []),
         scratch_shapes=[
             pltpu.VMEM((2, HALF, D), F32),
             pltpu.VMEM((2, HALF, D), F32),
@@ -755,8 +920,9 @@
             pltpu.VMEM((LAT, D), F32),
             pltpu.VMEM((2, LAT, HALF), BF),
             pltpu.VMEM((LAT, D), F32),
-        ],
-        compiler_params=params(),
+        ]
+        + (job.scratch() if direct else []),
+        compiler_params=params(collective_id=1, has_side_effects=True) if direct else params(),
         cost_estimate=cost(10 * rows * D * D, 14 * rows * D),
     )(
         output_grad,
@@ -772,13 +938,19 @@
         w_out_other,
         second_scale,
         second_shift,
+        *((g_down,) if direct else ()),
     )
 
     per_group = head_count // GROUPS
     width = per_group * HEAD
     group_heads = pl.BlockSpec((3, LAT, width), lambda g, i: (0, i, g))
-    d_heads, g_in, vec_in = pl.pallas_call(
-        attend_back_kernel,
+    group_job = Reduction(
+        D, 3 * width, tuple((n * width, (n + 1) * width) for n in range(3)), ORDERS
+    )
+    group_result = shape_of((D, 3 * width), BF)
+    jobs = [job, job, group_job] if direct else []
+    d_heads, g_in, vec_in, *more = pl.pallas_call(
+        functools.partial(attend_back_kernel, jobs, ATTEND_PLACES),
         grid=(GROUPS, images),
         name="attend_back",
         in_specs=[
@@ -788,28 +960,46 @@
             pl.BlockSpec((2, per_group, LAT, LAT), lambda g, i: (0, g, i, 0)),
             pl.BlockSpec((2, LAT, width), lambda g, i: (0, i, g)),
             pl.BlockSpec((LAT, HEAD), lambda g, i: (i, 0)),
-        ],
+        ]
+        + ([ANY] * 2 if direct else []),
         out_specs=[
             pl.BlockSpec((2, 3, LAT, width), lambda g, i: (0, 0, i, g)),
-            pl.BlockSpec((None, 2, D, 3 * width), lambda g, i: (g, 0, 0, 0)),
+            pl.BlockSpec(
+                (None, 2, D, 3 * width), lambda g, i: (0 if direct else g, 0, 0, 0)
+            ),
             pl.BlockSpec((None, 8, 6 * width), lambda g, i: (g, 0, 0)),
-        ],
+        ]
+        + [ANY] * len(jobs),
         out_shape=[
             shape_of((2, 3, rows, HALF), BF),
-            shape_of((GROUPS, 2, D, 3 * width), BF),
+            shape_of((1 if direct else GROUPS, 2, D, 3 * width), BF),
             shape_of((GROUPS, 8, 6 * width), F32),
-        ],
+        ]
+        + ([result, result, group_result] if direct else []),
         scratch_shapes=[
             pltpu.VMEM((D, 6 * width), F32),
             pltpu.VMEM((LAT, 6 * width), BF),
             pltpu.VMEM((LAT, HEAD), F32),
-        ],
-        compiler_params=params(),
+        ]
+        + ([pltpu.VMEM((D, 3 * width), BF)] if direct else [])
+        + sum([one.scratch() for one in jobs], []),
+        compiler_params=params(collective_id=2, has_side_effects=True) if direct else params(),
         cost_estimate=cost(8 * rows * D * D, 20 * rows * D),
-    )(normed_one, heads_own, heads_other, probs, d_mixed, d_dots)
-
-    latents_grad, vec_one = pl.pallas_call(
-        last_kernel,
+    )(
+        normed_one,
+        heads_own,
+        heads_other,
+        probs,
+        d_mixed,
+        d_dots,
+        *((g_up, g_out) if direct else ()),
+    )
+
+    stages = 1 + len(ORDERS[0])
+    grad_low, vectors, *last = pl.pallas_call(
+        functools.partial(
+            last_kernel, group_job if direct else None, LAST_PLACES, factor
+        ),
         grid=(images,),
         name="input_back",
         in_specs=[
@@ -819,97 +1009,115 @@
             whole_spec((3, D, HALF)),
             whole_spec((3, D, HALF)),
             vector,
-        ],
-        out_specs=[row_spec(D), kept_spec((8, D))],
-        out_shape=[shape_of((rows, D), F32), shape_of((8, D), F32)],
-        scratch_shapes=[pltpu.VMEM((LAT, D), F32)],
-        compiler_params=params(),
+            kept_spec((3, 8, D)),
+            kept_spec((8, D)),
+            kept_spec((2, 8, HALF)),
+            kept_spec((GROUPS, 8, 6 * width)),
+        ]
+        + ([ANY] if direct else []),
+        out_specs=[row_spec(D), kept_spec((16, D))] + ([ANY] if direct else []),
+        out_shape=[shape_of((rows, D), BF), shape_of((16, D), F32)]
+        + ([group_result] if direct else []),
+        scratch_shapes=[pltpu.VMEM((LAT, D), F32), pltpu.VMEM((2, 8, D), F32)]
+        + (
+            [
+                pltpu.VMEM((stages + 1, 16, D), F32),
+                pltpu.VMEM((stages, 16, D), F32),
+                pltpu.SemaphoreType.DMA((stages,)),
+                pltpu.SemaphoreType.DMA((stages,)),
+            ]
+            + group_job.scratch()
+            if direct
+            else []
+        ),
+        compiler_params=params(collective_id=3, has_side_effects=True) if direct else params(),
         cost_estimate=cost(6 * rows * D * D, 14 * rows * D),
-    )(latents, d_heads, d_middle, w_in_own, w_in_other, first_scale)
-
-    g_first_scale, g_first_shift = vec_one[0], vec_one[1]
-    g_second_scale, g_second_shift, g_output_bias = vec_two[0], vec_two[1], vec_two[2]
-    g_down_bias = g_sum[0]
-    by_group = vec_in[:, 0].reshape(GROUPS, 2, 3, width)
-    in_bias = jnp.transpose(by_group, (1, 2, 0, 3)).reshape(2, 3, HALF)
-    sharded = jnp.stack([in_bias[:, 0], in_bias[:, 2], vec_up[:2]], axis=1)
-
+    )(
+        latents,
+        d_heads,
+        d_middle,
+        w_in_own,
+        w_in_other,
+        first_scale,
+        vec_two,
+        g_sum,
+        vec_up,
+        vec_in,
+        *((g_in.reshape(2, D, 3 * width),) if direct else ()),
+    )
+
+    pieces = 8
+    cut = rows // pieces
     if direct:
-        me = lax.axis_index("mp")
-        sharded = jnp.where(me == 0, sharded, sharded[::-1])
-        sharded = jnp.transpose(sharded, (1, 0, 2)).reshape(3, D)
+        latents_grad, g_down, g_up, g_out, g_in = pl.pallas_call(
+            functools.partial(finish_kernel, factor),
+            grid=(pieces,),
+            name="finish",
+            in_specs=[
+                pl.BlockSpec((cut, D), lambda i: (i, 0)),
+                pl.BlockSpec((HALF // pieces, D), lambda i: (i, 0)),
+                pl.BlockSpec((HALF, D // pieces), lambda i: (0, i)),
+                pl.BlockSpec((HALF // pieces, D), lambda i: (i, 0)),
+                pl.BlockSpec((D // pieces, 3 * width), lambda i: (i, 0)),
+                pl.BlockSpec((D // pieces, 3 * width), lambda i: (i, 0)),
+            ],
+            out_specs=[
+                pl.BlockSpec((cut, D), lambda i: (i, 0)),
+                pl.BlockSpec((HALF // pieces, D), lambda i: (i, 0)),
+                pl.BlockSpec((D // pieces, HALF), lambda i: (i, 0)),
+                pl.BlockSpec((HALF // pieces, D), lambda i: (i, 0)),
+                pl.BlockSpec((3, D // pieces, HALF), lambda i: (0, i, 0)),
+            ],
+            out_shape=[
+                shape_of((rows, D), F32),
+                shape_of((HALF, D), F32),
+                shape_of((D, HALF), F32),
+                shape_of((HALF, D), F32),
+                shape_of((3, D, HALF), F32),
+            ],
+            compiler_params=params(),
+        )(grad_low, sums[0], more[0], more[1], more[2], last[0])
+        mine = vectors[6:9, :HALF]
     else:
-        sharded = jnp.transpose(sharded, (1, 0, 2)).reshape(3, D)
-    vectors = lax.psum(
-        jnp.concatenate(
-            [
-                jnp.stack(
-                    [
-                        g_first_scale,
-                        g_first_shift,
-                        g_output_bias,
-                        g_second_scale,
-                        g_second_shift,
-                        g_down_bias,
-                    ]
-                ),
-                sharded,
-            ]
-        ),
-        ("dp", "mp"),
-    )
-    vectors = vectors * factor
-    own_width = D // mp
-    mine = lax.dynamic_slice_in_dim(vectors[6:], lax.axis_index("mp") * own_width, own_width, 1)
-
-    if direct:
-        parts = ((0, 384), (384, 768), (768, 1024))
-        jobs = [
-            Reduction(HALF, D, parts, ORDERS),
-            Reduction(HALF, D, parts, ORDERS),
-            Reduction(HALF, D, parts, ORDERS),
-        ] + [
-            Reduction(D, 3 * width, ((0, width), (width, 2 * width), (2 * width, 3 * width)), ORDERS)
-        ] * GROUPS
-        sources = [g_down, g_up, g_out] + [g_in[g] for g in range(GROUPS)]
-        g_down, g_up, g_out, *g_in = pl.pallas_call(
-            functools.partial(reduce_kernel, jobs),
-            name="reduce",
-            in_specs=[ANY] * len(jobs),
-            out_specs=[ANY] * len(jobs),
-            out_shape=[shape_of((job.rows, job.columns), BF) for job in jobs],
-            scratch_shapes=sum([job.scratch() for job in jobs], [])
-            + [pltpu.SemaphoreType.DMA((len(jobs),))],
-            compiler_params=params(collective_id=1, has_side_effects=True),
-        )(*sources)
-        g_up = g_up.T
-        g_in = jnp.stack([part.reshape(D, 3, width) for part in g_in], axis=2)
-        g_in = jnp.transpose(g_in, (1, 0, 2, 3)).reshape(3, D, HALF)
-    else:
+        latents_grad = pl.pallas_call(
+            functools.partial(finish_kernel, factor),
+            grid=(pieces,),
+            name="finish",
+            in_specs=[pl.BlockSpec((cut, D), lambda i: (i, 0))],
+            out_specs=pl.BlockSpec((cut, D), lambda i: (i, 0)),
+            out_shape=shape_of((rows, D), F32),
+            compiler_params=params(),
+        )(grad_low)
+        vectors = lax.psum(vectors, ("dp", "mp")) * factor
+        own_width = D // mp
+        mine = lax.dynamic_slice_in_dim(
+            vectors[6:9], lax.axis_index("mp") * own_width, own_width, 1
+        )
         g_down, g_up, g_out = (v.reshape(D, D) for v in (g_down, g_up, g_out))
         g_in = jnp.transpose(g_in.reshape(GROUPS, 2, D, 3, width), (3, 2, 1, 0, 4))
         g_in = g_in.reshape(3, D, D)
-        scatter = lambda v, axis: lax.psum(
-            lax.psum_scatter(v, "mp", scatter_dimension=axis, tiled=True), "dp"
-        )
+
+        def scatter(v, axis):
+            v = lax.psum_scatter(v, "mp", scatter_dimension=axis, tiled=True)
+            return lax.psum(v, "dp").astype(F32) * factor
+
         g_down, g_up, g_out = scatter(g_down, 0), scatter(g_up.T, 1), scatter(g_out, 0)
         g_in = scatter(g_in, 2)
 
-    final = lambda v: v.astype(F32) * factor
     return (
         block_output,
         latents_grad,
         vectors[0],
         vectors[1],
-        final(g_in),
+        g_in,
         mine[:2],
-        final(g_out),
+        g_out,
         vectors[2],
         vectors[3],
         vectors[4],
-        final(g_up),
+        g_up,
         mine[2],
-        final(g_down),
+        g_down,
         vectors[5],
     )
 

time: 618 us -> 412 us (0.67); the launches traced: 608 us -> 411 us
  Pallas kernels: 527 us -> 403 us
  blocking collectives: 42.1 us -> 0 us
  local copies, waits for them, and re-layouts: 30 us -> 6.28 us
  other arithmetic: 8.21 us -> 1.36 us
    pallas_call x4, Pallas kernels: 409 us -> 284 us  [the longest x1 116 us: per_device(): pl.pallas_call(functools.partial(attend_back_kernel, jobs, ATTEND_PLACES)...]
    psum x1 -> x0, blocking collectives: 42.1 us -> none  [per_device(): lax.psum(jnp.concatenate([jnp.stack([g_first_scale, g_first_shift, g_outp...]
    unnamed x7 -> x2, local copies, waits for them, and re-layouts: 8.47 us -> 0.01 us
    mul x4 -> x0, other arithmetic: 6.83 us -> none  [the longest x3 6.82 us: per_device(): final = lambda v: v.astype(F32) * factor]
where the time goes in v2:
time: 412 us; the launch traced here: 411 us
  Pallas kernels  403 us (98%)
  local copies, waits for them, and re-layouts  6.28 us (2%)
    pallas_call x1, Pallas kernels, per_device(): pl.pallas_call(functools.partial(attend_back_kernel, jobs, ATTEND_PLACES)...  116 us
    pallas_call x1, Pallas kernels, per_device(): pl.pallas_call(forward_kernel, grid=(images,), name='forward', in_specs=[...  95.4 us
    pallas_call x1, Pallas kernels, per_device(): pl.pallas_call(functools.partial(feed_back_kernel, job, FEED_PLACES), gri...  79.4 us
    pallas_call x1, Pallas kernels, per_device(): pl.pallas_call(functools.partial(last_kernel, group_job if direct else No...  72.7 us
    pallas_call x1, Pallas kernels, per_device(): pl.pallas_call(functools.partial(first_kernel, direct), grid=(images,), n...  22.8 us
    pallas_call x1, Pallas kernels, per_device(): pl.pallas_call(functools.partial(finish_kernel, factor), grid=(pieces,),...  16.1 us

profile of v2, /device:TPU:0, one launch (start us, length us, event | category | flops | bytes accessed | tf_op | source)
XLA Modules:
  0.0 410.9 jit_solution(18161349372322967416)
XLA Ops:
  0.7 0.1 pad.2.clone
  0.7 0.7 broadcast_in_dim.26.ub_own
  1.4 0.0 copy-start
  1.4 1.4 maximum_maximum_fusion.bias_ref.refs_4_
  2.8 22.8 %project_own.1 = (bf16[4096,1024]{1,0:T(8,128)(2,1)}, bf16[3,4096,512]{2,1,0:T(8,128)(2,1)}, bf16[3,1024,512]{2,1,0:T(8,128)(2,1)}, bf16[512,1024]{1,0:T(8,128)(...) custom-call(bf16[4096,1024]{1,0:T(8,128)(2,1)} %x_ref.5, f32[1,1024]{1,0:T(1,128)} %bitcast.28, ...), custom_call_target="tpu_custom_call" | custom-call | flops 12884901888 | bytes 50331648 | tf_op jit(solution)/shard_map/project_own/pallas_call | solution.py:755
  25.6 0.0 copy-done
  25.6 1.3 slice.30.ub_other
  26.9 95.4 %forward.1 = (f32[4096,1024]{1,0:T(8,128)}, bf16[3,4096,512]{2,1,0:T(8,128)(2,1)}, bf16[2,4,4096,512]{3,2,1,0:T(8,128)(2,1)}, f32[4096,128]{1,0:T(8,128)}, bf16[...) custom-call(bf16[4096,1024]{1,0:T(8,128)(2,1)} %x_ref.5, ...), custom_call_target="tpu_custom_call" | custom-call | flops 68719476736 | bytes 100663296 | tf_op jit(solution)/shard_map/forward/pallas_call | solution.py:801
  122.2 79.4 %feed_back.1 = (bf16[4096,1024]{1,0:T(8,128)(2,1)}, bf16[2,4096,512]{2,1,0:T(8,128)(2,1)}, f32[4096,128]{1,0:T(8,128)}, bf16[2,512,1024]{2,1,0:T(8,128)(2,1)}, b...) custom-call(bf16[4096,1024]{1,0:T(8,128)(2,1)} %g_ref.3, ...), custom_call_target="tpu_custom_call" | custom-call | flops 42949672960 | bytes 58720256 | tf_op jit(solution)/shard_map/feed_back/pallas_call | solution.py:876
  201.6 116.2 %attend_back.1 = (bf16[2,3,4096,512]{3,2,1,0:T(8,128)(2,1)}, bf16[1,2,1024,768]{3,2,1,0:T(8,128)(2,1)}, f32[2,8,1536]{2,1,0:T(8,128)}, bf16[512,1024]{1,0:T(8,12...) custom-call(bf16[4096,1024]{1,0:T(8,128)(2,1)} %get-tuple-element.52.normed_ref, ...), custom_call_target="tpu_custom_call" | custom-call | flops 34359738368 | bytes 83886080 | tf_op jit(solution)/shard_map/attend_back/pallas_call | solution.py:952
  317.8 72.7 %input_back.1 = (bf16[4096,1024]{1,0:T(8,128)(2,1)}, f32[16,1024]{1,0:T(8,128)}, bf16[1024,768]{1,0:T(8,128)(2,1)}) custom-call(bf16[4096,1024]{1,0:T(8,128)(2,1)} %x_ref.5, bf16[2,3,4096,512]{3,2,1,0:T(8,128)(2,1)} %get-tuple-element.71.dheads_ref, bf16[4096,1024]{1,0:T(8,128)(2,1)} %get-tuple-element.72.dmid_ref, bf16[3,1024,512]{2,1,0:T(8,128)(2,1)} %w_own.1, ...), custom_call_target="tpu_custom_call" | custom-call | flops 25769803776 | bytes 58720256 | tf_op jit(solution)/shard_map/input_back/pallas_call | solution.py:999
  390.5 1.3 slice.37
  391.8 1.3 slice.33
  393.1 1.6 fusion
  394.7 16.1 %finish.1 = (f32[4096,1024]{1,0:T(8,128)}, f32[512,1024]{1,0:T(8,128)}, f32[1024,512]{1,0:T(8,128)}, f32[512,1024]{1,0:T(8,128)}, f32[3,1024,512]{2,1,0:T(8,128)}) custom-call(bf16[4096,1024]{1,0:T(8,128)(2,1)} %get-tuple-element.78.lat_ref, bf16[512,1024]{1,0:T(8,128)(2,1)} %get-tuple-element.79.refs_0_, bf16[512,1024]{1,0:T(8,128)(2,1)} %get-tuple-element.80.refs_1_, ...), custom_call_target="tpu_custom_call" | custom-call | tf_op jit(solution)/shard_map/finish/pallas_call | solution.py:1052
  (1 shorter events, 0.0 us)
Async XLA Ops:
  1.4 24.2 %copy-start = (bf16[1,512]{1,0:T(2,128)(2,1)}, bf16[1,512]{1,0:T(2,128)(2,1)S(1)}, u32[]{:S(2)}) copy-start(bf16[1,512]{1,0:T(2,128)(2,1)S(1)} %broadcast_in_dim.26.ub_own) | copy-start | bytes 3076
